TPU v7x, 32 devices: a whole 2x2x4 slice. The times are simulated.
32 devices in a mesh: dp: 4 (over z), row: 4 (over y, core), col: 2 (over x).
Axes of the slice: x: 2, y: 2, z: 4, core: 2. Of those that a mesh axis runs over, the one named last changes fastest.
Arguments:
- x_in: bfloat16 [2048, 1024], P(('dp', 'col'), 'row'), may hold values from -30 to 30
- norm_gain: float32 [1024], P('row'), may hold values from 0.1 to 1.9
- b_weight: bfloat16 [1024, 1024], P('row', 'col'), may hold values from -0.1875 to 0.1875
- c_weight: bfloat16 [1024, 1024], P('row', 'col'), may hold values from -0.1875 to 0.1875
- x_weight: bfloat16 [1024, 1024], P('row', 'col'), may hold values from -0.1875 to 0.1875
- conv_weight: float32 [3, 1024], P(None, 'col'), may hold values from -3 to 3
- out_weight: bfloat16 [1024, 1024], P('col', 'row'), may hold values from -0.1875 to 0.1875
- ffn_gain: float32 [1024], P('row'), may hold values from 0.1 to 1.9
- gate_weight: bfloat16 [1024, 4608], P('row', 'col'), may hold values from -0.1875 to 0.1875
- up_weight: bfloat16 [1024, 4608], P('row', 'col'), may hold values from -0.1875 to 0.1875
- down_weight: bfloat16 [4608, 1024], P('col', 'row'), may hold values from -0.1875 to 0.1875
- cotangent: bfloat16 [2048, 1024], P(('dp', 'col'), 'row'), may hold values from -16 to 16
Outputs:
- block_out: float32 [2048, 1024], P(('dp', 'col'), 'row')
- x_grad: float32 [2048, 1024], P(('dp', 'col'), 'row')
- norm_gain_grad: float32 [1024], P('row')
- b_weight_grad: float32 [1024, 1024], P('row', 'col')
- c_weight_grad: float32 [1024, 1024], P('row', 'col')
- x_weight_grad: float32 [1024, 1024], P('row', 'col')
- conv_weight_grad: float32 [3, 1024], P(None, 'col')
- out_weight_grad: float32 [1024, 1024], P('col', 'row')
- ffn_gain_grad: float32 [1024], P('row')
- gate_weight_grad: float32 [1024, 4608], P('row', 'col')
- up_weight_grad: float32 [1024, 4608], P('row', 'col')
- down_weight_grad: float32 [4608, 1024], P('col', 'row')
All inputs are finite; a program needn't handle non-finite values.
Results may differ from a plain program's by a relative error of at most 0.0081.
Values may be sent and summed in bfloat16 or wider, within the bound.
No kernel may reach another device: no remote copies, remote signals or barrier semaphores. Data moves between devices by JAX's collectives and lax.ppermute only.
A program may use at most 128 MiB of HBM per device.

v0:
```python
import functools

import jax
import jax.numpy as jnp
from jax import lax
from jax.experimental import pallas as pl
from jax.experimental.pallas import tpu as pltpu
from jax.sharding import PartitionSpec as P


LEN = 128
EPSILON = 1e-05
BF = jnp.bfloat16
F32 = jnp.float32


def dot_rows(left_side, right_side):
    return lax.dot_general(
        left_side, right_side, (((0,), (0,)), ((), ())), preferred_element_type=F32
    )


def dot_against(left_side, right_side):
    return lax.dot_general(
        left_side, right_side, (((1,), (1,)), ((), ())), preferred_element_type=F32
    )


def dot_plain(left_side, right_side):
    return jnp.dot(left_side, right_side, preferred_element_type=F32)


def pick(values, index, axis=0):
    return lax.dynamic_index_in_dim(values, index, axis, keepdims=False)


def row_steps(rows):
    return 2 if rows % 32 == 0 else 1


def split_kernel(count, width, row_ref, left_ref, right_ref, *out_refs):
    for row in range(count):

        @pl.when(row_ref[0] == row)
        def _(row=row):
            for k, out_ref in enumerate(out_refs):
                at = (row ^ k) * width
                out_ref[:, :width] = left_ref[:, at : at + width]
                out_ref[:, width:] = right_ref[:, at : at + width]


def split_columns(row, count, left, right):
    rows, columns = left.shape
    width = columns // count
    step = rows // row_steps(rows)
    return pl.pallas_call(
        functools.partial(split_kernel, count, width),
        grid=(rows // step,),
        in_specs=[
            pl.BlockSpec(memory_space=pltpu.SMEM),
            pl.BlockSpec((step, columns), lambda i: (i, 0)),
            pl.BlockSpec((step, columns), lambda i: (i, 0)),
        ],
        out_specs=[pl.BlockSpec((step, 2 * width), lambda i: (i, 0))] * count,
        out_shape=[jax.ShapeDtypeStruct((rows, 2 * width), left.dtype)] * count,
        cost_estimate=pl.CostEstimate(
            flops=0, transcendentals=0, bytes_accessed=4 * 2 * rows * columns
        ),
    )(row.reshape(1), left, right)


def nbytes(*arrays):
    return sum(a.size * a.dtype.itemsize for a in arrays)


def whole_call(kernel, row, arrays, shapes):
    out = pl.pallas_call(
        kernel,
        in_specs=[pl.BlockSpec(memory_space=pltpu.SMEM)]
        + [pl.BlockSpec(memory_space=pltpu.VMEM)] * len(arrays),
        out_specs=[pl.BlockSpec(memory_space=pltpu.VMEM)] * len(shapes),
        out_shape=shapes,
        cost_estimate=pl.CostEstimate(
            flops=0, transcendentals=0, bytes_accessed=nbytes(*arrays) + nbytes(*shapes)
        ),
    )(row.reshape(1), *arrays)
    return out


def first_kernel(chips, size, row_ref, own_ref, mate_ref, x_ref, cot_ref, one_ref, gain_ref):
    width = own_ref.shape[-1] // 2
    for at, (kr, kc) in enumerate(chips):
        for core, ref in ((0, own_ref), (1, mate_ref)):
            slot = row_ref[0] ^ (kr ^ core)
            where = pl.ds(pl.multiple_of(slot * width, width), width)
            x_ref[kc * size : (kc + 1) * size, where] = ref[at, 0:size, :width]
            cot_ref[kc * size : (kc + 1) * size, where] = ref[at, 0:size, width:]
            if kc == 0:
                parts = ref[at, size : size + 16, :].astype(F32)
                both = parts[0:1] + parts[1:2] + parts[2:3]
                gain_ref[0:1, where] = both[:, :width]
                gain_ref[1:2, where] = both[:, width:]
    rows, features = x_ref.shape
    step = min(64, rows)
    for start in range(0, rows, step):
        values = x_ref[start : start + step, :].astype(F32)
        total = jnp.sum(values * values, axis=1, keepdims=True)
        inverse = lax.rsqrt(total / features + EPSILON)
        one_ref[start : start + step, :] = (values * inverse * gain_ref[0:1, :]).astype(BF)


def join_kernel(count, width, row_ref, *refs):
    parts, (left_ref, right_ref) = refs[:count], refs[count:]
    for row in range(count):

        @pl.when(row_ref[0] == row)
        def _(row=row):
            for k, part in enumerate(parts):
                at = (row ^ k) * width
                left_ref[:, at : at + width] = part[:, :width].astype(F32)
                right_ref[:, at : at + width] = part[:, width:].astype(F32)


def join_columns(row, parts):
    count = len(parts)
    rows, double = parts[0].shape
    width = double // 2
    step = rows // row_steps(rows)
    out_block = pl.BlockSpec((step, count * width), lambda i: (i, 0))
    out_shape = jax.ShapeDtypeStruct((rows, count * width), F32)
    return pl.pallas_call(
        functools.partial(join_kernel, count, width),
        grid=(rows // step,),
        in_specs=[pl.BlockSpec(memory_space=pltpu.SMEM)]
        + [pl.BlockSpec((step, double), lambda i: (i, 0))] * count,
        out_specs=[out_block] * 2,
        out_shape=[out_shape] * 2,
        cost_estimate=pl.CostEstimate(
            flops=0, transcendentals=0, bytes_accessed=6 * count * rows * double
        ),
    )(row.reshape(1), *parts)


def mix_join_kernel(sizes, row_ref, z_ref, *refs):
    groups, count, deep, wide, _, spare_row, spare_lane = sizes
    parts = refs[:groups]
    b_ref, c_ref, x_ref, out_ref, conv_ref, gain_ref, held = refs[groups:]
    quarter = parts[0].shape[1]
    for i, part in enumerate(parts):
        start = pl.multiple_of((z_ref[0] ^ i) * quarter, quarter)
        held[:, pl.ds(start, quarter), :] = part[...]
    half = deep // 2
    gain = jnp.zeros((8, half), F32)
    for k in range(count):
        spare = held[k, spare_row : spare_row + 16, spare_lane : spare_lane + half]
        gain = gain + spare.astype(F32)[:8]
    gain_ref[...] = gain
    for row in range(count):

        @pl.when(row_ref[0] == row)
        def _(row=row):
            for k in range(count):
                at = (row ^ k) * wide
                for n, ref in enumerate((b_ref, c_ref, x_ref)):
                    block = held[k, :deep, n * wide : (n + 1) * wide]
                    ref[:, at : at + wide] = block.astype(F32)
                out_ref[at : at + wide, :] = held[k, deep : deep + wide, :deep].astype(F32)
                spare = held[k, spare_row : spare_row + 16, spare_lane : spare_lane + wide]
                conv_ref[:, at : at + wide] = spare.astype(F32)[:8]


def mix_join(row, z, parts, count, deep, wide, spare_row, spare_lane):
    groups = len(parts)
    quarter, lanes = parts[0].shape[1:]
    sizes = (groups, count, deep, wide, lanes, spare_row, spare_lane)
    shapes = [jax.ShapeDtypeStruct((deep, count * wide), F32)] * 3 + [
        jax.ShapeDtypeStruct((count * wide, deep), F32),
        jax.ShapeDtypeStruct((8, count * wide), F32),
        jax.ShapeDtypeStruct((8, deep // 2), F32),
    ]
    return pl.pallas_call(
        functools.partial(mix_join_kernel, sizes),
        in_specs=[pl.BlockSpec(memory_space=pltpu.SMEM)] * 2
        + [pl.BlockSpec(memory_space=pltpu.VMEM)] * groups,
        out_specs=[pl.BlockSpec(memory_space=pltpu.VMEM)] * 6,
        out_shape=shapes,
        scratch_shapes=[pltpu.VMEM((count, groups * quarter, lanes), BF)],
        cost_estimate=pl.CostEstimate(
            flops=0, transcendentals=0, bytes_accessed=nbytes(*parts) + nbytes(*shapes)
        ),
    )(row.reshape(1), z.reshape(1), *parts)


def causal_conv(values, kernel):
    channels = values.shape[1]
    padded = jnp.pad(values.reshape(-1, LEN, channels), ((0, 0), (2, 0), (0, 0)))
    result = kernel[0] * padded[:, :-2] + kernel[1] * padded[:, 1:-1] + kernel[2] * padded[:, 2:]
    return result.reshape(values.shape)


def conv_backward(mixed_rows, conv_delta, kernel):
    channels = mixed_rows.shape[1]
    mixed_seqs = jnp.pad(mixed_rows.reshape(-1, LEN, channels), ((0, 0), (2, 0), (0, 0)))
    delta_seqs = conv_delta.reshape(-1, LEN, channels)
    kernel_grad = jnp.stack(
        [
            jnp.sum(delta_seqs * mixed_seqs[:, :-2], axis=(0, 1)),
            jnp.sum(delta_seqs * mixed_seqs[:, 1:-1], axis=(0, 1)),
            jnp.sum(delta_seqs * mixed_seqs[:, 2:], axis=(0, 1)),
        ]
    )
    delta_padded = jnp.pad(delta_seqs, ((0, 0), (0, 2), (0, 0)))
    mixed_delta = (
        kernel[0] * delta_padded[:, 2:]
        + kernel[1] * delta_padded[:, 1:-1]
        + kernel[2] * delta_padded[:, :-2]
    )
    return kernel_grad, mixed_delta.reshape(mixed_rows.shape)


def solution(mesh):
    Z, R, C = mesh.shape["dp"], mesh.shape["row"], mesh.shape["col"]

    def swap_row(values, k):
        if k == 0:
            return values
        return lax.ppermute(values, "row", [(i, i ^ k) for i in range(R)])

    def swap_dp(values, k):
        if k == 0:
            return values
        return lax.ppermute(values, "dp", [(i, i ^ k) for i in range(Z)])

    def swap_plane(values, key):
        kr, kc = key
        moves = [
            (i * C + j, (i ^ kr) * C + (j ^ kc)) for i in range(R) for j in range(C)
        ]
        return lax.ppermute(values, ("row", "col"), moves)

    high = [(kr, 0) for kr in range(2, R, 2)]
    wide = [(0, kc) for kc in range(1, C)]
    if (R // 2) * C <= 4:
        chip_stages = [[(kr, kc) for kr in range(0, R, 2) for kc in range(C)][1:]]
    else:
        chip_stages = [high, wide]
    highs = [(0, 0)] + high
    chips = [(kr, kc) for kc in range(C) for kr in range(0, R, 2)]

    def xor(a, b):
        return (a[0] ^ b[0], a[1] ^ b[1])

    def after(values, *others):
        return lax.optimization_barrier((values, others))[0]

    def exchange(held, stages):
        held = dict(held)
        for stage in stages:
            names = list(held)
            payload = held[names[0]]
            if len(names) > 1:
                payload = jnp.stack([held[n] for n in names])
            for offset in stage:
                got = swap_plane(payload, offset)
                for at, name in enumerate(names):
                    held[xor(name, offset)] = got[at] if len(names) > 1 else got
        return held

    def with_mates(held, *gates):
        payload = jnp.stack([held[n] for n in chips])
        if gates:
            payload = after(payload, *gates)
        got = swap_plane(payload, (1, 0))
        held = dict(held)
        for at, name in enumerate(chips):
            held[xor(name, (1, 0))] = got[at]
        return held

    def local(
        x_in,
        norm_gain,
        b_weight,
        c_weight,
        x_weight,
        conv_weight,
        out_weight,
        ffn_gain,
        gate_weight,
        up_weight,
        down_weight,
        cotangent,
    ):
        z = lax.axis_index("dp")
        r = lax.axis_index("row")
        TB, FB = x_in.shape
        D = FB * R
        TP = TB // R
        MW = b_weight.shape[1] // R
        FW = gate_weight.shape[1] // R

        def choose(values, index):
            if len(values) == 1:
                return values[0]
            if len(values) <= 4:
                middle = len(values) // 2
                return jnp.where(
                    index < middle,
                    choose(values[:middle], index),
                    choose(values[middle:], index - middle),
                )
            return pick(jnp.stack(values), index)

        def in_row_order(get):
            return [choose([get(b ^ i) for i in range(R)], r) for b in range(R)]

        def token_rows(held):
            rows = []
            for kc in range(C):
                rows = rows + in_row_order(lambda k: held[(k, kc)])
            return jnp.concatenate(rows, axis=-2)

        def column_rows(held):
            rows = []
            for kc in range(C):
                rows.append(jnp.concatenate(in_row_order(lambda k: held[(k, kc)]), axis=-1))
            return jnp.concatenate(rows, axis=-2)

        def scatter_sum(values):
            width = values.shape[1]
            values = values.reshape(C, R // 2, 2, TP, width)
            keep = choose([values[:, :, 0], values[:, :, 1]], r % 2)
            send = choose([values[:, :, 1], values[:, :, 0]], r % 2)
            chip = keep + swap_plane(send.astype(BF), (1, 0)).astype(F32)
            pieces = {}
            for kc in range(C):
                for h in range(R // 2):
                    order = [chip[kc, i ^ h] for i in range(R // 2)]
                    pieces[(2 * h, kc)] = choose(order, r // 2)
            return add_chips(pieces)

        def add_chips(pieces):
            for at in range(len(chip_stages) - 1, -1, -1):
                left = [(0, 0)]
                for stage in chip_stages[:at]:
                    left = left + [xor(n, o) for o in stage for n in left]
                total = {n: pieces[n] for n in left}
                for offset in chip_stages[at]:
                    payload = jnp.stack([pieces[xor(n, offset)].astype(BF) for n in left])
                    got = swap_plane(payload, offset)
                    for i, n in enumerate(left):
                        total[n] = total[n] + got[i].astype(F32)
                pieces = total
            return pieces[(0, 0)]

        def grow(groups, offsets):
            names = [n for some, _ in groups for n in some]
            arrays = [array for _, array in groups]
            payload = jnp.concatenate(arrays) if len(arrays) > 1 else arrays[0]
            return [(names, payload)] + [
                ([xor(n, offset) for n in names], swap_plane(payload, offset))
                for offset in offsets
            ]

        def far_pieces(groups, *gates):
            groups = [(names, after(array, *gates)) for names, array in groups]
            mates = [
                ([xor(n, (1, 0)) for n in names], swap_plane(array, (1, 0)))
                for names, array in groups
            ]
            return {
                n: array[at] for names, array in groups + mates for at, n in enumerate(names)
            }

        gains = jnp.concatenate([norm_gain, ffn_gain])[None]
        part_a = lax.reduce_precision(gains, 8, 7)
        part_b = lax.reduce_precision(gains - part_a, 8, 7)
        part_c = gains - part_a - part_b
        gain_rows = jnp.concatenate([part_a, part_b, part_c]).astype(BF)
        gain_rows = jnp.pad(gain_rows, ((0, 13), (0, 0)))
        block = jnp.concatenate(
            [jnp.concatenate([x_in, cotangent], axis=1), gain_rows], axis=0
        )
        xc_held = exchange({(0, 0): block}, chip_stages)
        xc_own = jnp.stack([xc_held[n] for n in chips])
        xc_all = (xc_own, swap_plane(xc_own, (1, 0)))
        x_group, cot_group, normed_one, gain_all = whole_call(
            functools.partial(first_kernel, chips, TB),
            r,
            xc_all,
            [jax.ShapeDtypeStruct((C * TB, D), BF)] * 3 + [jax.ShapeDtypeStruct((8, D), F32)],
        )
        norm_all, ffn_all = gain_all[0], gain_all[1]
        own_in = lax.dynamic_slice(x_group, (r * TP, 0), (TP, D)).astype(F32)
        cot_own = lax.dynamic_slice(cot_group, (r * TP, 0), (TP, D)).astype(F32)

        MP = max(3 * MW, FB)
        mix_got = []
        for k in range(R):
            at = (r ^ k) * MW
            piece = jnp.concatenate(
                [lax.dynamic_slice(w, (0, at), (FB, MW)) for w in (b_weight, c_weight, x_weight)],
                axis=1,
            )
            low = lax.dynamic_slice(out_weight, (at, 0), (MW, FB))
            piece = jnp.concatenate(
                [jnp.pad(piece, ((0, 0), (0, MP - 3 * MW))), jnp.pad(low, ((0, 0), (0, MP - FB)))]
            )
            mix_got.append(swap_row(piece, k))
        taps = lax.dynamic_slice(conv_weight, (0, r * MW), (3, MW))
        in_w = jnp.concatenate(in_row_order(lambda k: mix_got[k][:FB, : 3 * MW]), axis=0)
        out_w = jnp.concatenate(in_row_order(lambda k: mix_got[k][FB:, :FB]), axis=1)

        down_got = []
        gu_got = split_columns(r, R, gate_weight, up_weight)
        gu_got = [swap_row(piece, k) for k, piece in enumerate(gu_got)]
        for k in range(R):
            piece = lax.dynamic_slice(down_weight, ((r ^ k) * FW, 0), (FW, FB))
            down_got.append(swap_row(piece, k))
        gu_w = jnp.concatenate(in_row_order(lambda k: gu_got[k]), axis=0)
        gu_w = lax.optimization_barrier(gu_w)
        down_w = jnp.concatenate(in_row_order(lambda k: down_got[k]), axis=1)
        down_w = lax.optimization_barrier(down_w)

        def mixer_forward(normed):
            sums = dot_plain(normed, in_w)
            b_sum, c_sum, x_sum = sums[:, :MW], sums[:, MW : 2 * MW], sums[:, 2 * MW :]
            mixed = b_sum * x_sum
            conv_out = causal_conv(mixed, taps)
            gated = (c_sum * conv_out).astype(BF)
            return normed, b_sum, c_sum, x_sum, mixed, conv_out, gated

        def mixer_backward(state, mix_delta):
            _, b_sum, c_sum, x_sum, mixed, conv_out, _ = state
            gated_delta = dot_against(mix_delta, out_w)
            c_delta = (gated_delta * conv_out).astype(BF)
            conv_part, mixed_delta = conv_backward(mixed, gated_delta * c_sum, taps)
            b_delta = (mixed_delta * x_sum).astype(BF)
            x_delta = (mixed_delta * b_sum).astype(BF)
            return jnp.concatenate([b_delta, c_delta, x_delta], axis=1), conv_part

        def feed_forward(two, cot):
            sums = dot_plain(two, gu_w)
            gate_sum, up_sum = sums[:, :FW], sums[:, FW:]
            sigmoid_gate = jax.nn.sigmoid(gate_sum)
            activation = (gate_sum * sigmoid_gate * up_sum).astype(BF)
            act_delta = dot_against(cot, down_w)
            gate_delta = (
                act_delta * up_sum * sigmoid_gate * (1.0 + gate_sum * (1.0 - sigmoid_gate))
            ).astype(BF)
            up_delta = (act_delta * gate_sum * sigmoid_gate).astype(BF)
            return activation, jnp.concatenate([gate_delta, up_delta], axis=1)

        state = mixer_forward(normed_one)
        hidden_part = dot_plain(state[-1], out_w)
        hidden = own_in + scatter_sum(hidden_part)
        inv_second = lax.rsqrt(jnp.mean(hidden * hidden, axis=1) + EPSILON)
        normed_two = (hidden * inv_second[:, None] * ffn_all[None, :]).astype(BF)
        two_held = exchange({(0, 0): normed_two}, chip_stages)
        two_group = token_rows(with_mates(two_held))
        act_group, delta_group = feed_forward(two_group, cot_group)
        two_part = dot_against(delta_group, gu_w)
        two_delta = scatter_sum(two_part)
        scaled = two_delta * ffn_all[None, :]
        average = jnp.mean(scaled * hidden, axis=1)
        hidden_delta = (
            cot_own
            + inv_second[:, None] * scaled
            - hidden * (inv_second * inv_second * inv_second * average)[:, None]
        )
        mix_own = hidden_delta.astype(BF)
        mix_held = exchange({(0, 0): mix_own}, chip_stages)
        mix_group = lax.optimization_barrier(token_rows(with_mates(mix_held)))
        in_delta, conv_part = mixer_backward(state, mix_group)
        one_part = dot_against(in_delta, in_w)
        in_grad = dot_rows(state[0], in_delta)
        out_grad = dot_rows(state[-1], mix_group)
        norm_part = jnp.sum(in_grad * in_w.astype(F32), axis=1) / norm_all
        ffn_part = jnp.sum(two_delta * hidden * inv_second[:, None], axis=0)
        corner = MP - FB >= max(MW, FB // 2) and MW >= 8
        extras = jnp.zeros((R, 8, max(MW, FB // 2)), F32)
        extras = jnp.concatenate(
            [
                jnp.pad(
                    jnp.broadcast_to(conv_part[None], (R, 3, MW)),
                    ((0, 0), (0, 0), (0, max(MW, FB // 2) - MW)),
                ),
                jnp.pad(
                    jnp.concatenate(
                        [norm_part.reshape(R, 2, FB // 2), ffn_part.reshape(R, 2, FB // 2)],
                        axis=1,
                    ),
                    ((0, 0), (0, 0), (0, max(MW, FB // 2) - FB // 2)),
                ),
            ],
            axis=1,
        )
        low = out_grad.reshape(MW, R, FB).transpose(1, 0, 2)
        top = jnp.pad(in_grad.reshape(R, FB, 3 * MW), ((0, 0), (0, 0), (0, MP - 3 * MW)))
        if corner:
            room = ((0, 0), (0, MW - 7), (0, MP - FB - extras.shape[2]))
            low = jnp.concatenate([low, jnp.pad(extras, room)], axis=2)
            packed = jnp.concatenate([top, low], axis=1)
        else:
            low = jnp.pad(low, ((0, 0), (0, 0), (0, MP - FB)))
            rows = -(FB + MW + 7) % (16 * Z) + 7
            extras = jnp.pad(extras, ((0, 0), (0, rows - 7), (0, MP - extras.shape[2])))
            packed = jnp.concatenate([top, low, extras], axis=1)
        quarter_rows = packed.shape[1] // Z
        packed = packed.reshape(R, Z, quarter_rows, MP)
        quarter = pick(packed, z, 1)
        for k in range(1, Z):
            got = swap_dp(pick(packed, z ^ k, 1).astype(BF), k)
            quarter = quarter + got.astype(F32)
        quarter = quarter.astype(BF)
        mine = jnp.stack([swap_row(pick(quarter, r ^ k), k) for k in range(R)])
        by_z = [swap_dp(mine, k) for k in range(Z)]
        block_part = dot_plain(after(act_group, packed), down_w)
        sums = scatter_sum(jnp.concatenate([one_part, block_part], axis=1))
        one_delta, block_own = sums[:, :D], sums[:, D:]
        inv_own = lax.rsqrt(jnp.mean(own_in * own_in, axis=1) + EPSILON)
        scaled = one_delta * norm_all[None, :]
        average = jnp.mean(scaled * own_in, axis=1)
        x_grad = (
            hidden_delta
            + inv_own[:, None] * scaled
            - own_in * (inv_own * inv_own * inv_own * average)[:, None]
        )
        ends = jnp.stack([hidden + block_own, x_grad])
        got = [
            swap_row(lax.dynamic_slice(ends, (0, 0, (r ^ k) * FB), (2, TP, FB)), k)
            for k in range(R)
        ]
        ends = jnp.concatenate(in_row_order(lambda k: got[k]), axis=1)

        payload = jnp.stack([xc_held[n][:TB, FB:] for n in highs])
        far = jnp.stack([swap_dp(payload, k) for k in range(1, Z)], axis=1)
        cot_groups = grow([(highs, far)], wide)
        far = jnp.stack([swap_dp(normed_two, k) for k in range(1, Z)])[None]
        two_groups = grow([([(0, 0)], far)], high)
        two_groups = grow(two_groups, wide)
        cot_far = column_rows(far_pieces(cot_groups, packed)).reshape(-1, D)
        two_far = token_rows(far_pieces(two_groups, packed)).reshape(-1, D)
        two_far, cot_far = after((two_far, cot_far), in_delta)
        act_far, delta_far = feed_forward(two_far, cot_far)
        dn_grad = dot_rows(act_group, cot_group) + dot_rows(act_far, cot_far)
        gu_grad = dot_rows(two_group, delta_group) + dot_rows(two_far, delta_far)
        gu_back, dn_back = [], []
        for k in range(R):
            to = r ^ k
            piece = lax.dynamic_slice(dn_grad, (0, to * FB), (FW, FB)).astype(BF)
            dn_back.append(swap_row(piece, k))
            piece = lax.dynamic_slice(gu_grad, (to * FB, 0), (FB, 2 * FW)).astype(BF)
            gu_back.append(swap_row(piece, k))

        def joined(parts, cut, axis):
            return jnp.concatenate(
                in_row_order(lambda k: cut(parts[k]).astype(F32)), axis=axis
            )

        gate_grad, up_grad = join_columns(r, gu_back)
        down_grad = joined(dn_back, lambda g: g, 0)
        spare = (FB, FB) if corner else (FB + MW, 0)
        b_grad, c_grad, x_weight_grad, out_grad, conv_grad, gain_rows = mix_join(
            r, z, by_z, R, FB, MW, *spare
        )
        conv_grad = conv_grad[:3]
        gain_part = gain_rows[3:7].reshape(2, FB)
        gain_sum = gain_part
        for kc in range(1, C):
            gain_sum = gain_sum + lax.ppermute(gain_part, "col", [(i, i ^ kc) for i in range(C)])

        return (
            ends[0],
            ends[1],
            gain_sum[0],
            b_grad,
            c_grad,
            x_weight_grad,
            conv_grad,
            out_grad,
            gain_sum[1],
            gate_grad,
            up_grad,
            down_grad,
        )

    placed = (
        P(("dp", "col"), "row"),
        P("row"),
        P("row", "col"),
        P("row", "col"),
        P("row", "col"),
        P(None, "col"),
        P("col", "row"),
        P("row"),
        P("row", "col"),
        P("row", "col"),
        P("col", "row"),
        P(("dp", "col"), "row"),
    )
    return jax.shard_map(
        local,
        mesh=mesh,
        in_specs=placed,
        out_specs=(
            P(("dp", "col"), "row"),
            P(("dp", "col"), "row"),
            P("row"),
            P("row", "col"),
            P("row", "col"),
            P("row", "col"),
            P(None, "col"),
            P("col", "row"),
            P("row"),
            P("row", "col"),
            P("row", "col"),
            P("col", "row"),
        ),
        check_vma=False,
    )
```

profile of v0, /device:TPU:0, one launch (start us, length us, event | category | flops | bytes accessed | tf_op | source)
XLA Modules:
  0.0 315.6 jit_solution(3263405232535094577)
XLA Ops:
  2.4 3.0 collective-permute-start.1
  5.4 1.5 collective-permute-start
  7.0 1.5 constant_dynamic-slice_fusion.13
  8.5 1.6 constant_dynamic-slice_fusion.19
  12.1 2.0 collective-permute-start.5
  14.8 1.6 fusion.29
  16.6 3.4 %collective-permute-done = bf16[272,512]{1,0:T(8,128)(2,1)S(1)} collective-permute-done((bf16[272,512]{1,0:T(8,128)(2,1)S(1)}, bf16[272,512]{1,0:T(8,128)(2,1)S(1)}, u32[]{:S(2)}, u32[]{:S(2)}) %collective-permute-start) | collective-permute-done | bytes 278560 | tf_op jit(solution)/shard_map/ppermute | solution.py:239
  23.3 2.5 collective-permute-start.12
  26.4 6.3 %collective-permute-done.6 = bf16[384,384]{1,0:T(8,128)(2,1)S(1)} collective-permute-done((bf16[384,384]{1,0:T(8,128)(2,1)}, bf16[384,384]{1,0:T(8,128)(2,1)S(1)}, u32[]{:S(2)}, u32[]{:S(2)}) %collective-permute-start.6) | collective-permute-done | bytes 294944 | tf_op jit(solution)/shard_map/ppermute | solution.py:227
  32.7 1.8 collective-permute-start.13
  34.5 1.6 select_select_fusion.19
  36.2 1.8 select_select_fusion.9
  37.9 1.9 select_select_fusion.11
  39.9 3.5 %shard_map.211 = (bf16[512,1024]{1,0:T(8,128)(2,1)}, bf16[512,1024]{1,0:T(8,128)(2,1)}, bf16[512,1024]{1,0:T(8,128)(2,1)}, f32[8,1024]{1,0:T(8,128)}) custom-call(s32[1]{0:T(128)} %bitcast.row_ref, bf16[4,272,512]{2,1,0:T(8,128)(2,1)} %copy-done.3, bf16[4,272,512]{2,1,0:T(8,128)(2,1)} %collective-permute-done.3.mate_ref), custom_call_target="tpu_custom_call" | custom-call | bytes 5406720 | tf_op jit(solution)/shard_map/pallas_call | solution.py:77
  43.4 2.1 fusion.78
  48.0 3.4 %shard_map.212 = (bf16[256,1152]{1,0:T(8,128)(2,1)}, bf16[256,1152]{1,0:T(8,128)(2,1)}, bf16[256,1152]{1,0:T(8,128)(2,1)}, bf16[256,1152]{1,0:T(8,128)(2,1)}) custom-call(s32[1]{0:T(128)} %bitcast.row_ref, bf16[256,2304]{1,0:T(8,128)(2,1)} %left_ref.1, bf16[256,2304]{1,0:T(8,128)(2,1)} %right_ref.1), custom_call_target="tpu_custom_call" | custom-call | bytes 4718592 | tf_op jit(solution)/shard_map/pallas_call | solution.py:56
  51.9 1.5 select_select_fusion.7
  55.4 3.1 collective-permute-start.10
  59.3 2.0 collective-permute-done.8
  61.3 3.2 %collective-permute-done.10 = bf16[1,64,1024]{2,1,0:T(8,128)(2,1)S(1)} collective-permute-done((bf16[1,64,1024]{2,1,0:T(8,128)(2,1)S(1)}, bf16[1,64,1024]{2,1,0:T(8,128)(2,1)S(1)}, u32[]{:S(2)}, u32[]{:S(2)}) %collective-permute-start.10) | collective-permute-done | bytes 131104 | tf_op jit(solution)/shard_map/ppermute | solution.py:239
  64.5 9.4 %collective-permute-done.9 = bf16[1,64,1024]{2,1,0:T(8,128)(2,1)S(1)} collective-permute-done((bf16[1,64,1024]{2,1,0:T(8,128)(2,1)S(1)}, bf16[1,64,1024]{2,1,0:T(8,128)(2,1)S(1)}, u32[]{:S(2)}, u32[]{:S(2)}) %collective-permute-start.9) | collective-permute-done | bytes 131104 | tf_op jit(solution)/shard_map/ppermute | solution.py:239
  75.4 1.5 collective-permute-start.15
  76.9 4.5 %collective-permute-done.16 = bf16[64,1024]{1,0:T(8,128)(2,1)S(1)} collective-permute-done((bf16[64,1024]{1,0:T(8,128)(2,1)S(1)}, bf16[64,1024]{1,0:T(8,128)(2,1)S(1)}, u32[]{:S(2)}, u32[]{:S(2)}) %collective-permute-start.16) | collective-permute-done | bytes 131104 | tf_op jit(solution)/shard_map/ppermute | solution.py:239
  82.2 9.2 %collective-permute-done.14 = bf16[64,1024]{1,0:T(8,128)(2,1)S(1)} collective-permute-done((bf16[64,1024]{1,0:T(8,128)(2,1)S(1)}, bf16[64,1024]{1,0:T(8,128)(2,1)S(1)}, u32[]{:S(2)}, u32[]{:S(2)}) %collective-permute-start.14) | collective-permute-done | bytes 131104 | tf_op jit(solution)/shard_map/ppermute | solution.py:239
  95.8 2.2 multiply_convert_fusion.6
  98.0 1.6 fusion.6
  100.0 1.6 collective-permute-done.21
  102.1 1.7 collective-permute-start.24
  103.8 1.7 collective-permute-start.23
  107.9 2.5 collective-permute-start.48
  112.1 1.6 collective-permute-start.27
  113.7 1.7 collective-permute-start.26
  115.7 1.7 collective-permute-done.48
  117.4 1.8 collective-permute-start.55
  119.1 9.3 %collective-permute-done.47 = bf16[64,1024]{1,0:T(8,128)(2,1)S(1)} collective-permute-done((bf16[64,1024]{1,0:T(8,128)(2,1)S(1)}, bf16[64,1024]{1,0:T(8,128)(2,1)S(1)}, u32[]{:S(2)}, u32[]{:S(2)}) %collective-permute-start.47) | collective-permute-done | bytes 131104 | tf_op jit(solution)/shard_map/ppermute | solution.py:232
  128.5 6.5 %collective-permute-start.53 = (bf16[2,256,256]{2,1,0:T(8,128)(2,1)S(1)}, bf16[2,256,256]{2,1,0:T(8,128)(2,1)S(1)}, u32[]{:S(2)}, u32[]{:S(2)}) collective-permute-start(bf16[2,256,256]{2,1,0:T(8,128)(2,1)S(1)} %pad_maximum_fusion.18), channel_id=1, source_target_pairs={{0,8},{8,0},{16,24},{24,16},{1,9},{9,1},{17,25},{25,17},{2,10},{10... | collective-permute-start | bytes 786440 | tf_op jit(solution)/shard_map/ppermute | solution.py:232
  135.9 8.2 %collective-permute-done.54 = bf16[2,256,256]{2,1,0:T(8,128)(2,1)S(1)} collective-permute-done((bf16[2,256,256]{2,1,0:T(8,128)(2,1)S(1)}, bf16[2,256,256]{2,1,0:T(8,128)(2,1)S(1)}, u32[]{:S(2)}, u32[]{:S(2)}) %collective-permute-start.54) | collective-permute-done | bytes 262176 | tf_op jit(solution)/shard_map/ppermute | solution.py:232
  145.9 1.7 collective-permute-start.51
  152.7 3.2 %collective-permute-start.37 = (bf16[4,96,384]{2,1,0:T(8,128)(2,1)S(1)}, bf16[4,96,384]{2,1,0:T(8,128)(2,1)S(1)}, u32[]{:S(2)}, u32[]{:S(2)}) collective-permute-start(bf16[4,96,384]{2,1,0:T(8,128)(2,1)S(1)} %get-tuple-element.84), channel_id=1, source_target_pairs={{0,16},{8,24},{16,0},{24,8},{1,17},{9,25},{17,1},{25,9},{2,18},{10... | collective-permute-start | bytes 884744 | tf_op jit(solution)/shard_map/ppermute | solution.py:232
  158.1 6.2 %collective-permute-done.36 = bf16[4,96,384]{2,1,0:T(8,128)(2,1)S(1)} collective-permute-done((bf16[4,96,384]{2,1,0:T(8,128)(2,1)S(1)}, bf16[4,96,384]{2,1,0:T(8,128)(2,1)S(1)}, u32[]{:S(2)}, u32[]{:S(2)}) %collective-permute-start.36) | collective-permute-done | bytes 294944 | tf_op jit(solution)/shard_map/ppermute | solution.py:232
  164.3 12.1 %collective-permute-done.37 = bf16[4,96,384]{2,1,0:T(8,128)(2,1)S(1)} collective-permute-done((bf16[4,96,384]{2,1,0:T(8,128)(2,1)S(1)}, bf16[4,96,384]{2,1,0:T(8,128)(2,1)S(1)}, u32[]{:S(2)}, u32[]{:S(2)}) %collective-permute-start.37) | collective-permute-done | bytes 294944 | tf_op jit(solution)/shard_map/ppermute | solution.py:232
  177.0 1.5 collective-permute-start.39
  182.0 1.9 collective-permute-start.44
  183.8 3.9 %collective-permute-start.43 = (bf16[4,96,384]{2,1,0:T(8,128)(2,1)S(1)}, bf16[4,96,384]{2,1,0:T(8,128)(2,1)}, u32[]{:S(2)}, u32[]{:S(2)}) collective-permute-start(bf16[4,96,384]{2,1,0:T(8,128)(2,1)S(1)} %pad_maximum_fusion.15.refs_0_), channel_id=1, source_target_pairs={{0,16},{8,24},{16,0},{24,8},{1,17},{9,25},{17,1},{25,9},{2,18},{10... | collective-permute-start | bytes 884744 | tf_op jit(solution)/shard_map/ppermute | solution.py:232
  187.8 2.5 pad_maximum_fusion
  190.3 3.5 %collective-permute-done.44.refs_3_ = bf16[4,96,384]{2,1,0:T(8,128)(2,1)S(1)} collective-permute-done((bf16[4,96,384]{2,1,0:T(8,128)(2,1)S(1)}, bf16[4,96,384]{2,1,0:T(8,128)(2,1)S(1)}, u32[]{:S(2)}, u32[]{:S(2)}) %collective-permute-start.44) | collective-permute-done | bytes 294944 | tf_op jit(solution)/shard_map/ppermute | solution.py:232
  194.6 17.4 %collective-permute-done.43.refs_2_ = bf16[4,96,384]{2,1,0:T(8,128)(2,1)} collective-permute-done((bf16[4,96,384]{2,1,0:T(8,128)(2,1)S(1)}, bf16[4,96,384]{2,1,0:T(8,128)(2,1)}, u32[]{:S(2)}, u32[]{:S(2)}) %collective-permute-start.43) | collective-permute-done | bytes 294944 | tf_op jit(solution)/shard_map/ppermute | solution.py:232
  212.7 2.9 shard_map.213
  216.7 2.4 fusion.5
  221.8 1.5 fusion.21
  223.3 1.5 select_bitcast_fusion.3
  233.1 4.0 %fusion.85 = f32[1536,1152]{0,1:T(8,128)S(1)} fusion(bf16[1536,1024]{1,0:T(8,128)(2,1)S(1)} %bitcast.451, bf16[1024,1152]{1,0:T(8,128)(2,1)S(1)} %copy-done.11), kind=kOutput, calls=%fused_computation.305 | convolution fusion | flops 3623878656 | bytes 12582912 | tf_op jit(solution)/shard_map/dot_general | solution.py:30
  237.1 3.4 %multiply_convert_fusion.2 = (bf16[1536,576]{0,1:T(8,128)(2,1)S(1)}, bf16[1536,576]{0,1:T(8,128)(2,1)S(1)}) fusion(f32[1536,1152]{0,1:T(8,128)S(1)} %fusion.85, bf16[1536,1024]{1,0:T(8,128)(2,1)S(1)} %bitcast.418, bf16[576,1024]{1,0:T(8,128)(2,1)S(1)} %copy-done.19), kind=kOutput, calls=%fused_computation.8 | convolution fusion | flops 1823440896 | bytes 14942208 | tf_op jit(solution)/shard_map/dot_general | solution.py:24
  240.6 4.3 %fusion = f32[1024,1152]{1,0:T(8,128)S(1)} fusion(bf16[1536,1024]{1,0:T(8,128)(2,1)S(1)} %bitcast.452, bf16[1536,576]{0,1:T(8,128)(2,1)S(1)} %get-tuple-element.73, bf16[1536,576]{0,1:T(8,128)(2,1)S(1)} %get-tuple-element.72), kind=kOutput, calls=%fused_computation.2 | convolution fusion | flops 3630956544 | bytes 11403264 | tf_op jit(solution)/shard_map/dot_general | solution.py:18
  244.9 1.6 convolution_add_fusion
  249.7 2.0 fusion.4
  255.5 27.3 %collective-permute-done.63 = bf16[576,256]{1,0:T(8,128)(2,1)S(1)} collective-permute-done((bf16[576,256]{1,0:T(8,128)(2,1)S(1)}, bf16[576,256]{1,0:T(8,128)(2,1)S(1)}, u32[]{:S(2)}, u32[]{:S(2)}) %collective-permute-start.63) | collective-permute-done | bytes 294944 | tf_op jit(solution)/shard_map/ppermute | solution.py:227
  282.8 1.5 collective-permute-start.30
  284.3 3.5 %collective-permute-done.64 = bf16[576,256]{1,0:T(8,128)(2,1)S(1)} collective-permute-done((bf16[576,256]{1,0:T(8,128)(2,1)S(1)}, bf16[576,256]{1,0:T(8,128)(2,1)S(1)}, u32[]{:S(2)}, u32[]{:S(2)}) %collective-permute-start.64) | collective-permute-done | bytes 294944 | tf_op jit(solution)/shard_map/ppermute | solution.py:227
  287.8 2.4 collective-permute-start.32
  291.7 6.1 %collective-permute-done.32 = bf16[1,64,2048]{2,1,0:T(8,128)(2,1)S(1)} collective-permute-done((bf16[1,64,2048]{2,1,0:T(8,128)(2,1)S(1)}, bf16[1,64,2048]{2,1,0:T(8,128)(2,1)S(1)}, u32[]{:S(2)}, u32[]{:S(2)}) %collective-permute-start.32) | collective-permute-done | bytes 262176 | tf_op jit(solution)/shard_map/ppermute | solution.py:239
  297.8 5.5 %collective-permute-done.31 = bf16[1,64,2048]{2,1,0:T(8,128)(2,1)S(1)} collective-permute-done((bf16[1,64,2048]{2,1,0:T(8,128)(2,1)S(1)}, bf16[1,64,2048]{2,1,0:T(8,128)(2,1)S(1)}, u32[]{:S(2)}, u32[]{:S(2)}) %collective-permute-start.31) | collective-permute-done | bytes 262176 | tf_op jit(solution)/shard_map/ppermute | solution.py:239
  308.0 1.6 pad_maximum_fusion.2
  310.5 3.7 %shard_map.214 = (f32[256,2304]{1,0:T(8,128)}, f32[256,2304]{1,0:T(8,128)}) custom-call(s32[1]{0:T(128)} %bitcast.row_ref, bf16[256,1152]{1,0:T(8,128)(2,1)} %get-tuple-element.79.refs_0_, bf16[256,1152]{1,0:T(8,128)(2,1)} %copy-done.30, bf16[256,1152]{1,0:T(8,128)(2,1)} %copy-done.29, bf16[256,1152]{1,0:T(8,128)(2,1)} %copy-done.28), custom_call_target="tpu_custom_call" | custom-call | bytes 7077888 | tf_op jit(solution)/shard_map/pallas_call | solution.py:131
  (331 shorter events, 68.1 us)
Async XLA Ops:
  2.4 14.0 %collective-permute-start.1 = (bf16[272,512]{1,0:T(8,128)(2,1)S(1)}, bf16[272,512]{1,0:T(8,128)(2,1)S(1)}, u32[]{:S(2)}, u32[]{:S(2)}) collective-permute-start(bf16[272,512]{1,0:T(8,128)(2,1)S(1)} %get-tuple-element.142), channel_id=1, source_target_pairs={{0,1},{1,0},{2,3},{3,2},{4,5},{5,4},{6,7},{7,6},{8,9},{9,8},{10,11... | collective-permute-start | bytes 835592 | tf_op jit(solution)/shard_map/ppermute | solution.py:239
  5.4 14.5 %collective-permute-start = (bf16[272,512]{1,0:T(8,128)(2,1)S(1)}, bf16[272,512]{1,0:T(8,128)(2,1)S(1)}, u32[]{:S(2)}, u32[]{:S(2)}) collective-permute-start(bf16[272,512]{1,0:T(8,128)(2,1)S(1)} %get-tuple-element.142), channel_id=1, source_target_pairs={{0,4},{1,5},{2,6},{3,7},{4,0},{5,1},{6,2},{7,3},{8,12},{9,13},{10,... | collective-permute-start | bytes 835592 | tf_op jit(solution)/shard_map/ppermute | solution.py:239
  7.0 13.0 %collective-permute-start.2 = (bf16[272,512]{1,0:T(8,128)(2,1)S(1)}, bf16[272,512]{1,0:T(8,128)(2,1)S(1)}, u32[]{:S(2)}, u32[]{:S(2)}) collective-permute-start(bf16[272,512]{1,0:T(8,128)(2,1)S(1)} %get-tuple-element.142), channel_id=1, source_target_pairs={{0,5},{1,4},{2,7},{3,6},{4,1},{5,0},{6,3},{7,2},{8,13},{9,12},{10,... | collective-permute-start | bytes 835592 | tf_op jit(solution)/shard_map/ppermute | solution.py:239
  12.1 14.3 %collective-permute-start.5 = (bf16[384,384]{1,0:T(8,128)(2,1)}, bf16[384,384]{1,0:T(8,128)(2,1)S(1)}, u32[]{:S(2)}, u32[]{:S(2)}) collective-permute-start(bf16[384,384]{1,0:T(8,128)(2,1)} %fusion.30), channel_id=1, source_target_pairs={{0,4},{2,6},{4,0},{6,2},{1,5},{3,7},{5,1},{7,3},{8,12},{10,14},{12... | collective-permute-start | bytes 884744 | tf_op jit(solution)/shard_map/ppermute | solution.py:227
  14.8 17.9 %collective-permute-start.6 = (bf16[384,384]{1,0:T(8,128)(2,1)}, bf16[384,384]{1,0:T(8,128)(2,1)S(1)}, u32[]{:S(2)}, u32[]{:S(2)}) collective-permute-start(bf16[384,384]{1,0:T(8,128)(2,1)} %fusion.31), channel_id=1, source_target_pairs={{0,6},{2,4},{4,2},{6,0},{1,7},{3,5},{5,3},{7,1},{8,14},{10,12},{12... | collective-permute-start | bytes 884744 | tf_op jit(solution)/shard_map/ppermute | solution.py:227
  16.4 18.1 %collective-permute-start.4 = (bf16[384,384]{1,0:T(8,128)(2,1)}, bf16[384,384]{1,0:T(8,128)(2,1)}, u32[]{:S(2)}, u32[]{:S(2)}) collective-permute-start(bf16[384,384]{1,0:T(8,128)(2,1)} %fusion.29), channel_id=1, source_target_pairs={{0,2},{2,0},{4,6},{6,4},{1,3},{3,1},{5,7},{7,5},{8,10},{10,8},{12,... | collective-permute-start | bytes 884744 | tf_op jit(solution)/shard_map/ppermute | solution.py:227
  22.1 17.8 %collective-permute-start.3 = (bf16[4,272,512]{2,1,0:T(8,128)(2,1)S(1)}, bf16[4,272,512]{2,1,0:T(8,128)(2,1)}, u32[]{:S(2)}, u32[]{:S(2)}) collective-permute-start(bf16[4,272,512]{2,1,0:T(8,128)(2,1)S(1)} %pad_maximum_fusion.5.own_ref), channel_id=1, source_target_pairs={{0,2},{1,3},{2,0},{3,1},{4,6},{5,7},{6,4},{7,5},{8,10},{9,11},{10,... | collective-permute-start | bytes 3342344 | tf_op jit(solution)/shard_map/ppermute | solution.py:239
  23.3 28.7 %collective-permute-start.12 = (bf16[576,256]{1,0:T(8,128)(2,1)}, bf16[576,256]{1,0:T(8,128)(2,1)}, u32[]{:S(2)}, u32[]{:S(2)}) collective-permute-start(bf16[576,256]{1,0:T(8,128)(2,1)} %get-tuple-element.108), channel_id=1, source_target_pairs={{0,4},{2,6},{4,0},{6,2},{1,5},{3,7},{5,1},{7,3},{8,12},{10,14},{12... | collective-permute-start | bytes 884744 | tf_op jit(solution)/shard_map/ppermute | solution.py:227
  26.4 25.5 %collective-permute-start.11 = (bf16[576,256]{1,0:T(8,128)(2,1)}, bf16[576,256]{1,0:T(8,128)(2,1)}, u32[]{:S(2)}, u32[]{:S(2)}) collective-permute-start(bf16[576,256]{1,0:T(8,128)(2,1)} %get-tuple-element.109), channel_id=1, source_target_pairs={{0,2},{2,0},{4,6},{6,4},{1,3},{3,1},{5,7},{7,5},{8,10},{10,8},{12,... | collective-permute-start | bytes 884744 | tf_op jit(solution)/shard_map/ppermute | solution.py:227
  32.7 19.2 %collective-permute-start.13 = (bf16[576,256]{1,0:T(8,128)(2,1)}, bf16[576,256]{1,0:T(8,128)(2,1)}, u32[]{:S(2)}, u32[]{:S(2)}) collective-permute-start(bf16[576,256]{1,0:T(8,128)(2,1)} %get-tuple-element.110), channel_id=1, source_target_pairs={{0,6},{2,4},{4,2},{6,0},{1,7},{3,5},{5,3},{7,1},{8,14},{10,12},{12... | collective-permute-start | bytes 884744 | tf_op jit(solution)/shard_map/ppermute | solution.py:227
  48.0 5.5 %collective-permute-start.7 = (bf16[2,2,64,1024]{3,2,1,0:T(8,128)(2,1)}, bf16[2,2,64,1024]{3,2,1,0:T(8,128)(2,1)}, u32[]{:S(2)}, u32[]{:S(2)}) collective-permute-start(bf16[2,2,64,1024]{3,2,1,0:T(8,128)(2,1)} %fusion.17), channel_id=1, source_target_pairs={{0,2},{1,3},{2,0},{3,1},{4,6},{5,7},{6,4},{7,5},{8,10},{9,11},{10,... | collective-permute-start | bytes 1572872 | tf_op jit(solution)/shard_map/ppermute | solution.py:239
  51.4 40.1 %collective-permute-start.18 = (bf16[256,1152]{1,0:T(8,128)(2,1)}, bf16[256,1152]{1,0:T(8,128)(2,1)}, u32[]{:S(2)}, u32[]{:S(2)}) collective-permute-start(bf16[256,1152]{1,0:T(8,128)(2,1)} %get-tuple-element.40), channel_id=1, source_target_pairs={{0,2},{2,0},{4,6},{6,4},{1,3},{3,1},{5,7},{7,5},{8,10},{10,8},{12,... | collective-permute-start | bytes 1769480 | tf_op jit(solution)/shard_map/ppermute | solution.py:227
  51.9 39.6 %collective-permute-start.19 = (bf16[256,1152]{1,0:T(8,128)(2,1)}, bf16[256,1152]{1,0:T(8,128)(2,1)S(1)}, u32[]{:S(2)}, u32[]{:S(2)}) collective-permute-start(bf16[256,1152]{1,0:T(8,128)(2,1)} %get-tuple-element.41), channel_id=1, source_target_pairs={{0,4},{2,6},{4,0},{6,2},{1,5},{3,7},{5,1},{7,3},{8,12},{10,14},{12... | collective-permute-start | bytes 1769480 | tf_op jit(solution)/shard_map/ppermute | solution.py:227
  54.9 6.4 %collective-permute-start.8 = (bf16[1,64,1024]{2,1,0:T(8,128)(2,1)S(1)}, bf16[1,64,1024]{2,1,0:T(8,128)(2,1)S(1)}, u32[]{:S(2)}, u32[]{:S(2)}) collective-permute-start(bf16[1,64,1024]{2,1,0:T(8,128)(2,1)S(1)} %get-tuple-element.124), channel_id=1, source_target_pairs={{0,1},{1,0},{2,3},{3,2},{4,5},{5,4},{6,7},{7,6},{8,9},{9,8},{10,11... | collective-permute-start | bytes 393224 | tf_op jit(solution)/shard_map/ppermute | solution.py:239
  55.4 9.2 %collective-permute-start.10 = (bf16[1,64,1024]{2,1,0:T(8,128)(2,1)S(1)}, bf16[1,64,1024]{2,1,0:T(8,128)(2,1)S(1)}, u32[]{:S(2)}, u32[]{:S(2)}) collective-permute-start(bf16[1,64,1024]{2,1,0:T(8,128)(2,1)S(1)} %get-tuple-element.125), channel_id=1, source_target_pairs={{0,5},{1,4},{2,7},{3,6},{4,1},{5,0},{6,3},{7,2},{8,13},{9,12},{10,... | collective-permute-start | bytes 393224 | tf_op jit(solution)/shard_map/ppermute | solution.py:239
  58.4 15.5 %collective-permute-start.9 = (bf16[1,64,1024]{2,1,0:T(8,128)(2,1)S(1)}, bf16[1,64,1024]{2,1,0:T(8,128)(2,1)S(1)}, u32[]{:S(2)}, u32[]{:S(2)}) collective-permute-start(bf16[1,64,1024]{2,1,0:T(8,128)(2,1)S(1)} %get-tuple-element.126), channel_id=1, source_target_pairs={{0,4},{1,5},{2,6},{3,7},{4,0},{5,1},{6,2},{7,3},{8,12},{9,13},{10,... | collective-permute-start | bytes 393224 | tf_op jit(solution)/shard_map/ppermute | solution.py:239
  61.3 30.2 %collective-permute-start.20 = (bf16[256,1152]{1,0:T(8,128)(2,1)S(1)}, bf16[256,1152]{1,0:T(8,128)(2,1)S(1)}, u32[]{:S(2)}, u32[]{:S(2)}) collective-permute-start(bf16[256,1152]{1,0:T(8,128)(2,1)S(1)} %copy-done.62), channel_id=1, source_target_pairs={{0,6},{2,4},{4,2},{6,0},{1,7},{3,5},{5,3},{7,1},{8,14},{10,12},{12... | collective-permute-start | bytes 1769480 | tf_op jit(solution)/shard_map/ppermute | solution.py:227
  75.2 6.3 %collective-permute-start.16 = (bf16[64,1024]{1,0:T(8,128)(2,1)S(1)}, bf16[64,1024]{1,0:T(8,128)(2,1)S(1)}, u32[]{:S(2)}, u32[]{:S(2)}) collective-permute-start(bf16[64,1024]{1,0:T(8,128)(2,1)S(1)} %multiply_convert_fusion.7), channel_id=1, source_target_pairs={{0,5},{1,4},{2,7},{3,6},{4,1},{5,0},{6,3},{7,2},{8,13},{9,12},{10,... | collective-permute-start | bytes 393224 | tf_op jit(solution)/shard_map/ppermute | solution.py:239
  75.4 6.7 %collective-permute-start.15 = (bf16[64,1024]{1,0:T(8,128)(2,1)S(1)}, bf16[64,1024]{1,0:T(8,128)(2,1)S(1)}, u32[]{:S(2)}, u32[]{:S(2)}) collective-permute-start(bf16[64,1024]{1,0:T(8,128)(2,1)S(1)} %multiply_convert_fusion.7), channel_id=1, source_target_pairs={{0,1},{1,0},{2,3},{3,2},{4,5},{5,4},{6,7},{7,6},{8,9},{9,8},{10,11... | collective-permute-start | bytes 393224 | tf_op jit(solution)/shard_map/ppermute | solution.py:239
  81.5 9.9 %collective-permute-start.14 = (bf16[64,1024]{1,0:T(8,128)(2,1)S(1)}, bf16[64,1024]{1,0:T(8,128)(2,1)S(1)}, u32[]{:S(2)}, u32[]{:S(2)}) collective-permute-start(bf16[64,1024]{1,0:T(8,128)(2,1)S(1)} %multiply_convert_fusion.7), channel_id=1, source_target_pairs={{0,4},{1,5},{2,6},{3,7},{4,0},{5,1},{6,2},{7,3},{8,12},{9,13},{10,... | collective-permute-start | bytes 393224 | tf_op jit(solution)/shard_map/ppermute | solution.py:239
  91.4 2.0 collective-permute-start.17
  102.0 8.3 %collective-permute-start.22 = (bf16[1,64,1024]{2,1,0:T(8,128)(2,1)S(1)}, bf16[1,64,1024]{2,1,0:T(8,128)(2,1)S(1)}, u32[]{:S(2)}, u32[]{:S(2)}) collective-permute-start(bf16[1,64,1024]{2,1,0:T(8,128)(2,1)S(1)} %get-tuple-element.121), channel_id=1, source_target_pairs={{0,1},{1,0},{2,3},{3,2},{4,5},{5,4},{6,7},{7,6},{8,9},{9,8},{10,11... | collective-permute-start | bytes 393224 | tf_op jit(solution)/shard_map/ppermute | solution.py:239
  102.1 8.7 %collective-permute-start.24 = (bf16[1,64,1024]{2,1,0:T(8,128)(2,1)S(1)}, bf16[1,64,1024]{2,1,0:T(8,128)(2,1)S(1)}, u32[]{:S(2)}, u32[]{:S(2)}) collective-permute-start(bf16[1,64,1024]{2,1,0:T(8,128)(2,1)S(1)} %get-tuple-element.122), channel_id=1, source_target_pairs={{0,5},{1,4},{2,7},{3,6},{4,1},{5,0},{6,3},{7,2},{8,13},{9,12},{10,... | collective-permute-start | bytes 393224 | tf_op jit(solution)/shard_map/ppermute | solution.py:239
  103.8 7.9 %collective-permute-start.23 = (bf16[1,64,1024]{2,1,0:T(8,128)(2,1)S(1)}, bf16[1,64,1024]{2,1,0:T(8,128)(2,1)S(1)}, u32[]{:S(2)}, u32[]{:S(2)}) collective-permute-start(bf16[1,64,1024]{2,1,0:T(8,128)(2,1)S(1)} %get-tuple-element.123), channel_id=1, source_target_pairs={{0,4},{1,5},{2,6},{3,7},{4,0},{5,1},{6,2},{7,3},{8,12},{9,13},{10,... | collective-permute-start | bytes 393224 | tf_op jit(solution)/shard_map/ppermute | solution.py:239
  106.5 8.9 %collective-permute-start.46 = (bf16[64,1024]{1,0:T(8,128)(2,1)S(1)}, bf16[64,1024]{1,0:T(8,128)(2,1)S(1)}, u32[]{:S(2)}, u32[]{:S(2)}) collective-permute-start(bf16[64,1024]{1,0:T(8,128)(2,1)S(1)} %multiply_convert_fusion.7), channel_id=1, source_target_pairs={{0,8},{8,0},{16,24},{24,16},{1,9},{9,1},{17,25},{25,17},{2,10},{10... | collective-permute-start | bytes 393224 | tf_op jit(solution)/shard_map/ppermute | solution.py:232
  107.9 9.5 %collective-permute-start.48 = (bf16[64,1024]{1,0:T(8,128)(2,1)S(1)}, bf16[64,1024]{1,0:T(8,128)(2,1)S(1)}, u32[]{:S(2)}, u32[]{:S(2)}) collective-permute-start(bf16[64,1024]{1,0:T(8,128)(2,1)S(1)} %multiply_convert_fusion.7), channel_id=1, source_target_pairs={{0,24},{8,16},{16,8},{24,0},{1,25},{9,17},{17,9},{25,1},{2,26},{10... | collective-permute-start | bytes 393224 | tf_op jit(solution)/shard_map/ppermute | solution.py:232
  110.4 18.1 %collective-permute-start.47 = (bf16[64,1024]{1,0:T(8,128)(2,1)S(1)}, bf16[64,1024]{1,0:T(8,128)(2,1)S(1)}, u32[]{:S(2)}, u32[]{:S(2)}) collective-permute-start(bf16[64,1024]{1,0:T(8,128)(2,1)S(1)} %multiply_convert_fusion.7), channel_id=1, source_target_pairs={{0,16},{8,24},{16,0},{24,8},{1,17},{9,25},{17,1},{25,9},{2,18},{10... | collective-permute-start | bytes 393224 | tf_op jit(solution)/shard_map/ppermute | solution.py:232
  112.1 16.4 %collective-permute-start.27 = (bf16[64,1024]{1,0:T(8,128)(2,1)S(1)}, bf16[64,1024]{1,0:T(8,128)(2,1)S(1)}, u32[]{:S(2)}, u32[]{:S(2)}) collective-permute-start(bf16[64,1024]{1,0:T(8,128)(2,1)S(1)} %fusion.74), channel_id=1, source_target_pairs={{0,5},{1,4},{2,7},{3,6},{4,1},{5,0},{6,3},{7,2},{8,13},{9,12},{10,... | collective-permute-start | bytes 393224 | tf_op jit(solution)/shard_map/ppermute | solution.py:239
  113.7 21.3 %collective-permute-start.26 = (bf16[64,1024]{1,0:T(8,128)(2,1)S(1)}, bf16[64,1024]{1,0:T(8,128)(2,1)S(1)}, u32[]{:S(2)}, u32[]{:S(2)}) collective-permute-start(bf16[64,1024]{1,0:T(8,128)(2,1)S(1)} %fusion.74), channel_id=1, source_target_pairs={{0,1},{1,0},{2,3},{3,2},{4,5},{5,4},{6,7},{7,6},{8,9},{9,8},{10,11... | collective-permute-start | bytes 393224 | tf_op jit(solution)/shard_map/ppermute | solution.py:239
  115.4 19.6 %collective-permute-start.25 = (bf16[64,1024]{1,0:T(8,128)(2,1)S(1)}, bf16[64,1024]{1,0:T(8,128)(2,1)S(1)}, u32[]{:S(2)}, u32[]{:S(2)}) collective-permute-start(bf16[64,1024]{1,0:T(8,128)(2,1)S(1)} %fusion.74), channel_id=1, source_target_pairs={{0,4},{1,5},{2,6},{3,7},{4,0},{5,1},{6,2},{7,3},{8,12},{9,13},{10,... | collective-permute-start | bytes 393224 | tf_op jit(solution)/shard_map/ppermute | solution.py:239
  117.4 18.6 %collective-permute-start.55 = (bf16[2,256,256]{2,1,0:T(8,128)(2,1)S(1)}, bf16[2,256,256]{2,1,0:T(8,128)(2,1)S(1)}, u32[]{:S(2)}, u32[]{:S(2)}) collective-permute-start(bf16[2,256,256]{2,1,0:T(8,128)(2,1)S(1)} %pad_maximum_fusion.18), channel_id=1, source_target_pairs={{0,24},{8,16},{16,8},{24,0},{1,25},{9,17},{17,9},{25,1},{2,26},{10... | collective-permute-start | bytes 786440 | tf_op jit(solution)/shard_map/ppermute | solution.py:232
  128.4 15.8 %collective-permute-start.54 = (bf16[2,256,256]{2,1,0:T(8,128)(2,1)S(1)}, bf16[2,256,256]{2,1,0:T(8,128)(2,1)S(1)}, u32[]{:S(2)}, u32[]{:S(2)}) collective-permute-start(bf16[2,256,256]{2,1,0:T(8,128)(2,1)S(1)} %pad_maximum_fusion.18), channel_id=1, source_target_pairs={{0,16},{8,24},{16,0},{24,8},{1,17},{9,25},{17,1},{25,9},{2,18},{10... | collective-permute-start | bytes 786440 | tf_op jit(solution)/shard_map/ppermute | solution.py:232
  128.5 15.7 %collective-permute-start.53 = (bf16[2,256,256]{2,1,0:T(8,128)(2,1)S(1)}, bf16[2,256,256]{2,1,0:T(8,128)(2,1)S(1)}, u32[]{:S(2)}, u32[]{:S(2)}) collective-permute-start(bf16[2,256,256]{2,1,0:T(8,128)(2,1)S(1)} %pad_maximum_fusion.18), channel_id=1, source_target_pairs={{0,8},{8,0},{16,24},{24,16},{1,9},{9,1},{17,25},{25,17},{2,10},{10... | collective-permute-start | bytes 786440 | tf_op jit(solution)/shard_map/ppermute | solution.py:232
  135.0 9.7 %collective-permute-start.49 = (bf16[1,3,64,1024]{3,2,1,0:T(8,128)(2,1)S(1)}, bf16[1,3,64,1024]{3,2,1,0:T(8,128)(2,1)}, u32[]{:S(2)}, u32[]{:S(2)}) collective-permute-start(bf16[1,3,64,1024]{3,2,1,0:T(8,128)(2,1)S(1)} %maximum_bitcast_fusion), channel_id=1, source_target_pairs={{0,4},{1,5},{2,6},{3,7},{4,0},{5,1},{6,2},{7,3},{8,12},{9,13},{10,... | collective-permute-start | bytes 1179656 | tf_op jit(solution)/shard_map/ppermute | solution.py:239
  135.9 11.7 %collective-permute-start.28 = (bf16[4,64,1024]{2,1,0:T(8,128)(2,1)}, bf16[4,64,1024]{2,1,0:T(8,128)(2,1)S(1)}, u32[]{:S(2)}, u32[]{:S(2)}) collective-permute-start(bf16[4,64,1024]{2,1,0:T(8,128)(2,1)} %pad_maximum_fusion.12), channel_id=1, source_target_pairs={{0,2},{1,3},{2,0},{3,1},{4,6},{5,7},{6,4},{7,5},{8,10},{9,11},{10,... | collective-permute-start | bytes 1572872 | tf_op jit(solution)/shard_map/ppermute | solution.py:239
  144.4 43.4 %collective-permute-start.57 = (bf16[2,3,256,256]{3,2,1,0:T(8,128)(2,1)S(1)}, bf16[2,3,256,256]{3,2,1,0:T(8,128)(2,1)}, u32[]{:S(2)}, u32[]{:S(2)}) collective-permute-start(bf16[2,3,256,256]{3,2,1,0:T(8,128)(2,1)S(1)} %copy.58), channel_id=1, source_target_pairs={{0,1},{1,0},{2,3},{3,2},{4,5},{5,4},{6,7},{7,6},{8,9},{9,8},{10,11... | collective-permute-start | bytes 2359304 | tf_op jit(solution)/shard_map/ppermute | solution.py:239
  145.9 44.5 %collective-permute-start.51 = (bf16[2,3,64,1024]{3,2,1,0:T(8,128)(2,1)S(1)}, bf16[2,3,64,1024]{3,2,1,0:T(8,128)(2,1)S(1)}, u32[]{:S(2)}, u32[]{:S(2)}) collective-permute-start(bf16[2,3,64,1024]{3,2,1,0:T(8,128)(2,1)S(1)} %pad_maximum_fusion.7), channel_id=1, source_target_pairs={{0,1},{1,0},{2,3},{3,2},{4,5},{5,4},{6,7},{7,6},{8,9},{9,8},{10,11... | collective-permute-start | bytes 2359304 | tf_op jit(solution)/shard_map/ppermute | solution.py:239
  152.6 11.6 %collective-permute-start.36 = (bf16[4,96,384]{2,1,0:T(8,128)(2,1)S(1)}, bf16[4,96,384]{2,1,0:T(8,128)(2,1)S(1)}, u32[]{:S(2)}, u32[]{:S(2)}) collective-permute-start(bf16[4,96,384]{2,1,0:T(8,128)(2,1)S(1)} %get-tuple-element.83), channel_id=1, source_target_pairs={{0,8},{8,0},{16,24},{24,16},{1,9},{9,1},{17,25},{25,17},{2,10},{10... | collective-permute-start | bytes 884744 | tf_op jit(solution)/shard_map/ppermute | solution.py:232
  152.7 23.7 %collective-permute-start.37 = (bf16[4,96,384]{2,1,0:T(8,128)(2,1)S(1)}, bf16[4,96,384]{2,1,0:T(8,128)(2,1)S(1)}, u32[]{:S(2)}, u32[]{:S(2)}) collective-permute-start(bf16[4,96,384]{2,1,0:T(8,128)(2,1)S(1)} %get-tuple-element.84), channel_id=1, source_target_pairs={{0,16},{8,24},{16,0},{24,8},{1,17},{9,25},{17,1},{25,9},{2,18},{10... | collective-permute-start | bytes 884744 | tf_op jit(solution)/shard_map/ppermute | solution.py:232
  155.9 20.5 %collective-permute-start.38 = (bf16[4,96,384]{2,1,0:T(8,128)(2,1)S(1)}, bf16[4,96,384]{2,1,0:T(8,128)(2,1)S(1)}, u32[]{:S(2)}, u32[]{:S(2)}) collective-permute-start(bf16[4,96,384]{2,1,0:T(8,128)(2,1)S(1)} %get-tuple-element.85), channel_id=1, source_target_pairs={{0,24},{8,16},{16,8},{24,0},{1,25},{9,17},{17,9},{25,1},{2,26},{10... | collective-permute-start | bytes 884744 | tf_op jit(solution)/shard_map/ppermute | solution.py:232
  176.6 4.0 %collective-permute-start.41 = (bf16[96,384]{1,0:T(8,128)(2,1)S(1)}, bf16[96,384]{1,0:T(8,128)(2,1)S(1)}, u32[]{:S(2)}, u32[]{:S(2)}) collective-permute-start(bf16[96,384]{1,0:T(8,128)(2,1)S(1)} %get-tuple-element.138), channel_id=1, source_target_pairs={{0,6},{2,4},{4,2},{6,0},{1,7},{3,5},{5,3},{7,1},{8,14},{10,12},{12... | collective-permute-start | bytes 221192 | tf_op jit(solution)/shard_map/ppermute | solution.py:227
  176.7 5.2 %collective-permute-start.40 = (bf16[96,384]{1,0:T(8,128)(2,1)S(1)}, bf16[96,384]{1,0:T(8,128)(2,1)S(1)}, u32[]{:S(2)}, u32[]{:S(2)}) collective-permute-start(bf16[96,384]{1,0:T(8,128)(2,1)S(1)} %get-tuple-element.139), channel_id=1, source_target_pairs={{0,4},{2,6},{4,0},{6,2},{1,5},{3,7},{5,1},{7,3},{8,12},{10,14},{12... | collective-permute-start | bytes 221192 | tf_op jit(solution)/shard_map/ppermute | solution.py:227
  177.0 4.9 %collective-permute-start.39 = (bf16[96,384]{1,0:T(8,128)(2,1)S(1)}, bf16[96,384]{1,0:T(8,128)(2,1)S(1)}, u32[]{:S(2)}, u32[]{:S(2)}) collective-permute-start(bf16[96,384]{1,0:T(8,128)(2,1)S(1)} %get-tuple-element.140), channel_id=1, source_target_pairs={{0,2},{2,0},{4,6},{6,4},{1,3},{3,1},{5,7},{7,5},{8,10},{10,8},{12,... | collective-permute-start | bytes 221192 | tf_op jit(solution)/shard_map/ppermute | solution.py:227
  180.6 39.9 %collective-permute-start.56 = (bf16[2,3,256,256]{3,2,1,0:T(8,128)(2,1)}, bf16[2,3,256,256]{3,2,1,0:T(8,128)(2,1)}, u32[]{:S(2)}, u32[]{:S(2)}) collective-permute-start(bf16[2,3,256,256]{3,2,1,0:T(8,128)(2,1)} %copy.49), channel_id=1, source_target_pairs={{0,2},{1,3},{2,0},{3,1},{4,6},{5,7},{6,4},{7,5},{8,10},{9,11},{10,... | collective-permute-start | bytes 2359304 | tf_op jit(solution)/shard_map/ppermute | solution.py:239
  182.0 11.9 %collective-permute-start.44 = (bf16[4,96,384]{2,1,0:T(8,128)(2,1)S(1)}, bf16[4,96,384]{2,1,0:T(8,128)(2,1)S(1)}, u32[]{:S(2)}, u32[]{:S(2)}) collective-permute-start(bf16[4,96,384]{2,1,0:T(8,128)(2,1)S(1)} %pad_maximum_fusion.15.refs_0_), channel_id=1, source_target_pairs={{0,24},{8,16},{16,8},{24,0},{1,25},{9,17},{17,9},{25,1},{2,26},{10... | collective-permute-start | bytes 884744 | tf_op jit(solution)/shard_map/ppermute | solution.py:232
  183.8 28.1 %collective-permute-start.43 = (bf16[4,96,384]{2,1,0:T(8,128)(2,1)S(1)}, bf16[4,96,384]{2,1,0:T(8,128)(2,1)}, u32[]{:S(2)}, u32[]{:S(2)}) collective-permute-start(bf16[4,96,384]{2,1,0:T(8,128)(2,1)S(1)} %pad_maximum_fusion.15.refs_0_), channel_id=1, source_target_pairs={{0,16},{8,24},{16,0},{24,8},{1,17},{9,25},{17,1},{25,9},{2,18},{10... | collective-permute-start | bytes 884744 | tf_op jit(solution)/shard_map/ppermute | solution.py:232
  187.7 24.2 %collective-permute-start.42 = (bf16[4,96,384]{2,1,0:T(8,128)(2,1)S(1)}, bf16[4,96,384]{2,1,0:T(8,128)(2,1)S(1)}, u32[]{:S(2)}, u32[]{:S(2)}) collective-permute-start(bf16[4,96,384]{2,1,0:T(8,128)(2,1)S(1)} %pad_maximum_fusion.15.refs_0_), channel_id=1, source_target_pairs={{0,8},{8,0},{16,24},{24,16},{1,9},{9,1},{17,25},{25,17},{2,10},{10... | collective-permute-start | bytes 884744 | tf_op jit(solution)/shard_map/ppermute | solution.py:232
  190.3 33.0 %collective-permute-start.58 = (bf16[2,3,256,256]{3,2,1,0:T(8,128)(2,1)}, bf16[2,3,256,256]{3,2,1,0:T(8,128)(2,1)}, u32[]{:S(2)}, u32[]{:S(2)}) collective-permute-start(bf16[2,3,256,256]{3,2,1,0:T(8,128)(2,1)} %collective-permute-done.57), channel_id=1, source_target_pairs={{0,2},{1,3},{2,0},{3,1},{4,6},{5,7},{6,4},{7,5},{8,10},{9,11},{10,... | collective-permute-start | bytes 2359304 | tf_op jit(solution)/shard_map/ppermute | solution.py:239
  193.8 31.0 %collective-permute-start.50 = (bf16[2,3,64,1024]{3,2,1,0:T(8,128)(2,1)S(1)}, bf16[2,3,64,1024]{3,2,1,0:T(8,128)(2,1)}, u32[]{:S(2)}, u32[]{:S(2)}) collective-permute-start(bf16[2,3,64,1024]{3,2,1,0:T(8,128)(2,1)S(1)} %pad_maximum_fusion.7), channel_id=1, source_target_pairs={{0,2},{1,3},{2,0},{3,1},{4,6},{5,7},{6,4},{7,5},{8,10},{9,11},{10,... | collective-permute-start | bytes 2359304 | tf_op jit(solution)/shard_map/ppermute | solution.py:239
  211.9 18.9 %collective-permute-start.52 = (bf16[2,3,64,1024]{3,2,1,0:T(8,128)(2,1)S(1)}, bf16[2,3,64,1024]{3,2,1,0:T(8,128)(2,1)S(1)}, u32[]{:S(2)}, u32[]{:S(2)}) collective-permute-start(bf16[2,3,64,1024]{3,2,1,0:T(8,128)(2,1)S(1)} %collective-permute-done.51), channel_id=1, source_target_pairs={{0,2},{1,3},{2,0},{3,1},{4,6},{5,7},{6,4},{7,5},{8,10},{9,11},{10,... | collective-permute-start | bytes 2359304 | tf_op jit(solution)/shard_map/ppermute | solution.py:239
  216.3 3.6 %collective-permute-start.45 = (f32[2,256]{1,0:T(2,128)S(1)}, f32[2,256]{1,0:T(2,128)S(1)}, u32[]{:S(2)}, u32[]{:S(2)}) collective-permute-start(f32[2,256]{1,0:T(2,128)S(1)} %reshape.555), channel_id=1, source_target_pairs={{0,1},{1,0},{2,3},{3,2},{4,5},{5,4},{6,7},{7,6},{8,9},{9,8},{10,11... | collective-permute-start | bytes 6152 | tf_op jit(solution)/shard_map/ppermute | solution.py:570
  219.9 34.2 %collective-permute-start.29 = (bf16[2,2,64,2048]{3,2,1,0:T(8,128)(2,1)S(1)}, bf16[2,2,64,2048]{3,2,1,0:T(8,128)(2,1)S(1)}, u32[]{:S(2)}, u32[]{:S(2)}) collective-permute-start(bf16[2,2,64,2048]{3,2,1,0:T(8,128)(2,1)S(1)} %fusion.5), channel_id=1, source_target_pairs={{0,2},{1,3},{2,0},{3,1},{4,6},{5,7},{6,4},{7,5},{8,10},{9,11},{10,... | collective-permute-start | bytes 3145736 | tf_op jit(solution)/shard_map/ppermute | solution.py:239
  247.6 59.9 %collective-permute-start.61 = (bf16[256,1152]{1,0:T(8,128)(2,1)S(1)}, bf16[256,1152]{1,0:T(8,128)(2,1)S(1)}, u32[]{:S(2)}, u32[]{:S(2)}) collective-permute-start(bf16[256,1152]{1,0:T(8,128)(2,1)S(1)} %get-tuple-element.76), channel_id=1, source_target_pairs={{0,6},{2,4},{4,2},{6,0},{1,7},{3,5},{5,3},{7,1},{8,14},{10,12},{12... | collective-permute-start | bytes 1769480 | tf_op jit(solution)/shard_map/ppermute | solution.py:227
  249.0 60.6 %collective-permute-start.60 = (bf16[256,1152]{1,0:T(8,128)(2,1)S(1)}, bf16[256,1152]{1,0:T(8,128)(2,1)S(1)}, u32[]{:S(2)}, u32[]{:S(2)}) collective-permute-start(bf16[256,1152]{1,0:T(8,128)(2,1)S(1)} %get-tuple-element.77), channel_id=1, source_target_pairs={{0,4},{2,6},{4,0},{6,2},{1,5},{3,7},{5,1},{7,3},{8,12},{10,14},{12... | collective-permute-start | bytes 1769480 | tf_op jit(solution)/shard_map/ppermute | solution.py:227
  252.7 30.1 %collective-permute-start.63 = (bf16[576,256]{1,0:T(8,128)(2,1)S(1)}, bf16[576,256]{1,0:T(8,128)(2,1)S(1)}, u32[]{:S(2)}, u32[]{:S(2)}) collective-permute-start(bf16[576,256]{1,0:T(8,128)(2,1)S(1)} %get-tuple-element.105), channel_id=1, source_target_pairs={{0,4},{2,6},{4,0},{6,2},{1,5},{3,7},{5,1},{7,3},{8,12},{10,14},{12... | collective-permute-start | bytes 884744 | tf_op jit(solution)/shard_map/ppermute | solution.py:227
  254.1 33.7 %collective-permute-start.64 = (bf16[576,256]{1,0:T(8,128)(2,1)S(1)}, bf16[576,256]{1,0:T(8,128)(2,1)S(1)}, u32[]{:S(2)}, u32[]{:S(2)}) collective-permute-start(bf16[576,256]{1,0:T(8,128)(2,1)S(1)} %get-tuple-element.106), channel_id=1, source_target_pairs={{0,6},{2,4},{4,2},{6,0},{1,7},{3,5},{5,3},{7,1},{8,14},{10,12},{12... | collective-permute-start | bytes 884744 | tf_op jit(solution)/shard_map/ppermute | solution.py:227
  254.1 36.1 %collective-permute-start.62 = (bf16[576,256]{1,0:T(8,128)(2,1)S(1)}, bf16[576,256]{1,0:T(8,128)(2,1)S(1)}, u32[]{:S(2)}, u32[]{:S(2)}) collective-permute-start(bf16[576,256]{1,0:T(8,128)(2,1)S(1)} %get-tuple-element.107), channel_id=1, source_target_pairs={{0,2},{2,0},{4,6},{6,4},{1,3},{3,1},{5,7},{7,5},{8,10},{10,8},{12,... | collective-permute-start | bytes 884744 | tf_op jit(solution)/shard_map/ppermute | solution.py:227
  282.8 8.7 %collective-permute-start.30 = (bf16[1,64,2048]{2,1,0:T(8,128)(2,1)S(1)}, bf16[1,64,2048]{2,1,0:T(8,128)(2,1)S(1)}, u32[]{:S(2)}, u32[]{:S(2)}) collective-permute-start(bf16[1,64,2048]{2,1,0:T(8,128)(2,1)S(1)} %get-tuple-element.91), channel_id=1, source_target_pairs={{0,1},{1,0},{2,3},{3,2},{4,5},{5,4},{6,7},{7,6},{8,9},{9,8},{10,11... | collective-permute-start | bytes 786440 | tf_op jit(solution)/shard_map/ppermute | solution.py:239
  287.8 10.0 %collective-permute-start.32 = (bf16[1,64,2048]{2,1,0:T(8,128)(2,1)S(1)}, bf16[1,64,2048]{2,1,0:T(8,128)(2,1)S(1)}, u32[]{:S(2)}, u32[]{:S(2)}) collective-permute-start(bf16[1,64,2048]{2,1,0:T(8,128)(2,1)S(1)} %get-tuple-element.92), channel_id=1, source_target_pairs={{0,5},{1,4},{2,7},{3,6},{4,1},{5,0},{6,3},{7,2},{8,13},{9,12},{10,... | collective-permute-start | bytes 786440 | tf_op jit(solution)/shard_map/ppermute | solution.py:239
  290.2 13.1 %collective-permute-start.31 = (bf16[1,64,2048]{2,1,0:T(8,128)(2,1)S(1)}, bf16[1,64,2048]{2,1,0:T(8,128)(2,1)S(1)}, u32[]{:S(2)}, u32[]{:S(2)}) collective-permute-start(bf16[1,64,2048]{2,1,0:T(8,128)(2,1)S(1)} %get-tuple-element.93), channel_id=1, source_target_pairs={{0,4},{1,5},{2,6},{3,7},{4,0},{5,1},{6,2},{7,3},{8,12},{9,13},{10,... | collective-permute-start | bytes 786440 | tf_op jit(solution)/shard_map/ppermute | solution.py:239
  291.5 18.0 %collective-permute-start.59 = (bf16[256,1152]{1,0:T(8,128)(2,1)S(1)}, bf16[256,1152]{1,0:T(8,128)(2,1)S(1)}, u32[]{:S(2)}, u32[]{:S(2)}) collective-permute-start(bf16[256,1152]{1,0:T(8,128)(2,1)S(1)} %get-tuple-element.78), channel_id=1, source_target_pairs={{0,2},{2,0},{4,6},{6,4},{1,3},{3,1},{5,7},{7,5},{8,10},{10,8},{12,... | collective-permute-start | bytes 1769480 | tf_op jit(solution)/shard_map/ppermute | solution.py:227
  305.7 8.5 %collective-permute-start.35 = (f32[2,64,256]{2,1,0:T(8,128)S(1)}, f32[2,64,256]{2,1,0:T(8,128)S(1)}, u32[]{:S(2)}, u32[]{:S(2)}) collective-permute-start(f32[2,64,256]{2,1,0:T(8,128)S(1)} %get-tuple-element.134), channel_id=1, source_target_pairs={{0,6},{2,4},{4,2},{6,0},{1,7},{3,5},{5,3},{7,1},{8,14},{10,12},{12... | collective-permute-start | bytes 393224 | tf_op jit(solution)/shard_map/ppermute | solution.py:227
  307.0 7.3 %collective-permute-start.33 = (f32[2,64,256]{2,1,0:T(8,128)S(1)}, f32[2,64,256]{2,1,0:T(8,128)S(1)}, u32[]{:S(2)}, u32[]{:S(2)}) collective-permute-start(f32[2,64,256]{2,1,0:T(8,128)S(1)} %get-tuple-element.135), channel_id=1, source_target_pairs={{0,2},{2,0},{4,6},{6,4},{1,3},{3,1},{5,7},{7,5},{8,10},{10,8},{12,... | collective-permute-start | bytes 393224 | tf_op jit(solution)/shard_map/ppermute | solution.py:227
  307.4 7.0 %collective-permute-start.34 = (f32[2,64,256]{2,1,0:T(8,128)S(1)}, f32[2,64,256]{2,1,0:T(8,128)S(1)}, u32[]{:S(2)}, u32[]{:S(2)}) collective-permute-start(f32[2,64,256]{2,1,0:T(8,128)S(1)} %get-tuple-element.136), channel_id=1, source_target_pairs={{0,4},{2,6},{4,0},{6,2},{1,5},{3,7},{5,1},{7,3},{8,12},{10,14},{12... | collective-permute-start | bytes 393224 | tf_op jit(solution)/shard_map/ppermute | solution.py:227
  (68 other events, 358.5 us)
where the time goes:
time: 321 us; the launch traced here: 316 us
  waiting for transfers between devices  144 us (45%)
  starting transfers between devices  63.7 us (20%)
  other arithmetic  44.9 us (14%)
  matrix products  27.2 us (8%)
  local copies, waits for them, and re-layouts  19.6 us (6%)
  Pallas kernels  13.5 us (4%)
    ppermute x12, waiting for transfers between devices, swap_dp(): return lax.ppermute(values, 'dp', [(i, i ^ k) for i in range(Z)])  58.4 us
    ppermute x31, waiting for transfers between devices, swap_plane(): return lax.ppermute(values, ('row', 'col'), moves)  46.3 us
    ppermute x21, waiting for transfers between devices, swap_row(): return lax.ppermute(values, 'row', [(i, i ^ k) for i in range(R)])  39.6 us
    ppermute x31, starting transfers between devices, swap_plane(): return lax.ppermute(values, ('row', 'col'), moves)  24.9 us
    ppermute x12, starting transfers between devices, swap_dp(): return lax.ppermute(values, 'dp', [(i, i ^ k) for i in range(Z)])  22.9 us
    ppermute x21, starting transfers between devices, swap_row(): return lax.ppermute(values, 'row', [(i, i ^ k) for i in range(R)])  15.6 us
    select_n x12, other arithmetic, choose(): jnp.where(index < middle, choose(values[:middle], index), choose(values[m...  13.1 us
    dot_general x6, matrix products, dot_rows(): lax.dot_general(left_side, right_side, (((0,), (0,)), ((), ())), preferre...  9.9 us
  transfers between devices with their start and end apart: 65, of which 26 were waited for; matrix products, arithmetic and copies ran while one was open for 24% of the time, Pallas kernels for 4%

commit v1 on v0

--- a/solution.py
+++ b/solution.py
@@ -38,15 +38,31 @@
     return 2 if rows % 32 == 0 else 1
 
 
+def by_chunks(rows, body, step=16):
+    step = step if rows % step == 0 else rows
+
+    def run(i, carry):
+        body(pl.ds(pl.multiple_of(i * step, step), step))
+        return carry
+
+    if step == rows:
+        body(slice(0, rows))
+    else:
+        lax.fori_loop(0, rows // step, run, 0)
+
+
 def split_kernel(count, width, row_ref, left_ref, right_ref, *out_refs):
     for row in range(count):
 
         @pl.when(row_ref[0] == row)
         def _(row=row):
-            for k, out_ref in enumerate(out_refs):
-                at = (row ^ k) * width
-                out_ref[:, :width] = left_ref[:, at : at + width]
-                out_ref[:, width:] = right_ref[:, at : at + width]
+            def body(where):
+                for k, out_ref in enumerate(out_refs):
+                    at = (row ^ k) * width
+                    out_ref[where, :width] = left_ref[where, at : at + width]
+                    out_ref[where, width:] = right_ref[where, at : at + width]
+
+            by_chunks(left_ref.shape[0], body)
 
 
 def split_columns(row, count, left, right):
@@ -69,6 +85,48 @@
     )(row.reshape(1), left, right)
 
 
+def ffn_kernel(width, two_ref, cot_ref, gu_ref, down_ref, act_ref, delta_ref):
+    sums = dot_plain(two_ref[...], gu_ref[...])
+    act_delta = dot_against(cot_ref[...], down_ref[...])
+    gate_sum, up_sum = sums[:, :width], sums[:, width:]
+    sigmoid_gate = jax.nn.sigmoid(gate_sum)
+    silu = gate_sum * sigmoid_gate
+    act_ref[...] = (silu * up_sum).astype(BF)
+    slope = sigmoid_gate * (1.0 + gate_sum * (1.0 - sigmoid_gate))
+    delta_ref[:, :width] = (act_delta * up_sum * slope).astype(BF)
+    delta_ref[:, width:] = (act_delta * silu).astype(BF)
+
+
+def ffn_call(two, cot, gu_w, down_w):
+    rows, features = two.shape
+    width = down_w.shape[0]
+    tile = 256 if rows % 256 == 0 else rows
+    tokens = pl.BlockSpec((tile, features), lambda i: (i, 0))
+    return pl.pallas_call(
+        functools.partial(ffn_kernel, width),
+        grid=(rows // tile,),
+        in_specs=[
+            tokens,
+            tokens,
+            pl.BlockSpec(gu_w.shape, lambda i: (0, 0)),
+            pl.BlockSpec(down_w.shape, lambda i: (0, 0)),
+        ],
+        out_specs=[
+            pl.BlockSpec((tile, width), lambda i: (i, 0)),
+            pl.BlockSpec((tile, 2 * width), lambda i: (i, 0)),
+        ],
+        out_shape=[
+            jax.ShapeDtypeStruct((rows, width), BF),
+            jax.ShapeDtypeStruct((rows, 2 * width), BF),
+        ],
+        cost_estimate=pl.CostEstimate(
+            flops=6 * rows * features * width,
+            transcendentals=rows * width,
+            bytes_accessed=2 * (2 * rows * features + 3 * features * width + 3 * rows * width),
+        ),
+    )(two, cot, gu_w, down_w)
+
+
 def nbytes(*arrays):
     return sum(a.size * a.dtype.itemsize for a in arrays)
 
@@ -101,12 +159,14 @@
                 gain_ref[0:1, where] = both[:, :width]
                 gain_ref[1:2, where] = both[:, width:]
     rows, features = x_ref.shape
-    step = min(64, rows)
-    for start in range(0, rows, step):
-        values = x_ref[start : start + step, :].astype(F32)
+
+    def normalize(where):
+        values = x_ref[where, :].astype(F32)
         total = jnp.sum(values * values, axis=1, keepdims=True)
         inverse = lax.rsqrt(total / features + EPSILON)
-        one_ref[start : start + step, :] = (values * inverse * gain_ref[0:1, :]).astype(BF)
+        one_ref[where, :] = (values * inverse * gain_ref[0:1, :]).astype(BF)
+
+    by_chunks(rows, normalize, 64)
 
 
 def join_kernel(count, width, row_ref, *refs):
@@ -115,10 +175,13 @@
 
         @pl.when(row_ref[0] == row)
         def _(row=row):
-            for k, part in enumerate(parts):
-                at = (row ^ k) * width
-                left_ref[:, at : at + width] = part[:, :width].astype(F32)
-                right_ref[:, at : at + width] = part[:, width:].astype(F32)
+            def body(where):
+                for k, part in enumerate(parts):
+                    at = (row ^ k) * width
+                    left_ref[where, at : at + width] = part[where, :width].astype(F32)
+                    right_ref[where, at : at + width] = part[where, width:].astype(F32)
+
+            by_chunks(left_ref.shape[0], body)
 
 
 def join_columns(row, parts):
@@ -161,9 +224,13 @@
         def _(row=row):
             for k in range(count):
                 at = (row ^ k) * wide
-                for n, ref in enumerate((b_ref, c_ref, x_ref)):
-                    block = held[k, :deep, n * wide : (n + 1) * wide]
-                    ref[:, at : at + wide] = block.astype(F32)
+
+                def body(where, k=k, at=at):
+                    for n, ref in enumerate((b_ref, c_ref, x_ref)):
+                        block = held[k, where, n * wide : (n + 1) * wide]
+                        ref[where, at : at + wide] = block.astype(F32)
+
+                by_chunks(deep, body)
                 out_ref[at : at + wide, :] = held[k, deep : deep + wide, :deep].astype(F32)
                 spare = held[k, spare_row : spare_row + 16, spare_lane : spare_lane + wide]
                 conv_ref[:, at : at + wide] = spare.astype(F32)[:8]
@@ -541,7 +608,7 @@
         cot_far = column_rows(far_pieces(cot_groups, packed)).reshape(-1, D)
         two_far = token_rows(far_pieces(two_groups, packed)).reshape(-1, D)
         two_far, cot_far = after((two_far, cot_far), in_delta)
-        act_far, delta_far = feed_forward(two_far, cot_far)
+        act_far, delta_far = ffn_call(two_far, cot_far, gu_w, down_w)
         dn_grad = dot_rows(act_group, cot_group) + dot_rows(act_far, cot_far)
         gu_grad = dot_rows(two_group, delta_group) + dot_rows(two_far, delta_far)
         gu_back, dn_back = [], []

time: 321 us -> 330 us (1.028)
  Pallas kernels: 13.5 us -> 27.4 us
  starting transfers between devices: 63.7 us -> 70.4 us
  matrix products: 27.2 us -> 21.9 us
  waiting for transfers between devices: 144 us -> 140 us
    ppermute x12, waiting for transfers between devices: 58.4 us -> 44.6 us  [swap_dp(): return lax.ppermute(values, 'dp', [(i, i ^ k) for i in range(Z)])]
    pallas_call x0 -> x1, Pallas kernels: none -> 11.8 us  [ffn_call(): pl.pallas_call(functools.partial(ffn_kernel, width), grid=(rows // tile,)...]
    ppermute x31, waiting for transfers between devices: 46.3 us -> 56.9 us  [swap_plane(): return lax.ppermute(values, ('row', 'col'), moves)]
    ppermute x31, starting transfers between devices: 24.9 us -> 33.9 us  [swap_plane(): return lax.ppermute(values, ('row', 'col'), moves)]
    unnamed x21, other arithmetic: 7.55 us -> 3.13 us
    dot_general x5 -> x4, matrix products: 8.98 us -> 4.83 us  [dot_plain(): return jnp.dot(left_side, right_side, preferred_element_type=F32)]
    dot_general x5 -> x4, matrix products: 8.35 us -> 4.88 us  [dot_against(): lax.dot_general(left_side, right_side, (((1,), (1,)), ((), ())), preferre...]
    unnamed x134 -> x158, local copies, waits for them, and re-layouts: 7.36 us -> 10.5 us
  transfers between devices with their start and end apart: 65 -> 65, of which waited for: 26 -> 29; matrix products, arithmetic and copies ran while one was open for 24% -> 20% of each run, Pallas kernels for 4% -> 8%
where the time goes in v1:
time: 330 us; the launch traced here: 326 us
  waiting for transfers between devices  140 us (42%)
  starting transfers between devices  70.4 us (21%)
  other arithmetic  41.7 us (13%)
  Pallas kernels  27.4 us (8%)
  local copies, waits for them, and re-layouts  22.9 us (7%)
  matrix products  21.9 us (7%)
    ppermute x31, waiting for transfers between devices, swap_plane(): return lax.ppermute(values, ('row', 'col'), moves)  56.9 us
    ppermute x12, waiting for transfers between devices, swap_dp(): return lax.ppermute(values, 'dp', [(i, i ^ k) for i in range(Z)])  44.6 us
    ppermute x21, waiting for transfers between devices, swap_row(): return lax.ppermute(values, 'row', [(i, i ^ k) for i in range(R)])  38.5 us
    ppermute x31, starting transfers between devices, swap_plane(): return lax.ppermute(values, ('row', 'col'), moves)  33.9 us
    ppermute x12, starting transfers between devices, swap_dp(): return lax.ppermute(values, 'dp', [(i, i ^ k) for i in range(Z)])  21.8 us
    ppermute x21, starting transfers between devices, swap_row(): return lax.ppermute(values, 'row', [(i, i ^ k) for i in range(R)])  14.1 us
    dot_general x6, matrix products, dot_rows(): lax.dot_general(left_side, right_side, (((0,), (0,)), ((), ())), preferre...  12.2 us
    pallas_call x1, Pallas kernels, ffn_call(): pl.pallas_call(functools.partial(ffn_kernel, width), grid=(rows // tile,)...  11.8 us
  transfers between devices with their start and end apart: 65, of which 29 were waited for; matrix products, arithmetic and copies ran while one was open for 20% of the time, Pallas kernels for 8%

profile of v1, /device:TPU:0, one launch (start us, length us, event | category | flops | bytes accessed | tf_op | source)
XLA Modules:
  0.0 326.3 jit_solution(11646130462286890862)
XLA Ops:
  2.4 4.0 %collective-permute-start.2 = (bf16[272,512]{1,0:T(8,128)(2,1)S(1)}, bf16[272,512]{1,0:T(8,128)(2,1)S(1)}, u32[]{:S(2)}, u32[]{:S(2)}) collective-permute-start(bf16[272,512]{1,0:T(8,128)(2,1)S(1)} %get-tuple-element.144), channel_id=1, source_target_pairs={{0,5},{1,4},{2,7},{3,6},{4,1},{5,0},{6,3},{7,2},{8,13},{9,12},{10,... | collective-permute-start | bytes 835592 | tf_op jit(solution)/shard_map/ppermute | solution.py:306
  8.0 1.6 constant_dynamic-slice_fusion.19
  15.1 4.3 %collective-permute-done.1 = bf16[272,512]{1,0:T(8,128)(2,1)S(1)} collective-permute-done((bf16[272,512]{1,0:T(8,128)(2,1)S(1)}, bf16[272,512]{1,0:T(8,128)(2,1)S(1)}, u32[]{:S(2)}, u32[]{:S(2)}) %collective-permute-start.1) | collective-permute-done | bytes 278560 | tf_op jit(solution)/shard_map/ppermute | solution.py:306
  21.4 1.5 collective-permute-start.12
  23.0 2.4 collective-permute-done.6
  26.8 5.1 %collective-permute-done.5 = bf16[384,384]{1,0:T(8,128)(2,1)} collective-permute-done((bf16[384,384]{1,0:T(8,128)(2,1)}, bf16[384,384]{1,0:T(8,128)(2,1)}, u32[]{:S(2)}, u32[]{:S(2)}) %collective-permute-start.5) | collective-permute-done | bytes 294944 | tf_op jit(solution)/shard_map/ppermute | solution.py:294
  31.9 1.7 select_select_fusion.19
  37.4 4.4 %shard_map.211 = (bf16[512,1024]{1,0:T(8,128)(2,1)}, bf16[512,1024]{1,0:T(8,128)(2,1)}, bf16[512,1024]{1,0:T(8,128)(2,1)}, f32[8,1024]{1,0:T(8,128)}) custom-call(s32[1]{0:T(128)} %bitcast.row_ref, bf16[4,272,512]{2,1,0:T(8,128)(2,1)} %copy-done.4, bf16[4,272,512]{2,1,0:T(8,128)(2,1)} %copy-done.17), custom_call_target="tpu_custom_call" | custom-call | bytes 5406720 | tf_op jit(solution)/shard_map/pallas_call | solution.py:135
  41.8 2.0 fusion.71
  46.5 3.8 %shard_map.212 = (bf16[256,1152]{1,0:T(8,128)(2,1)}, bf16[256,1152]{1,0:T(8,128)(2,1)}, bf16[256,1152]{1,0:T(8,128)(2,1)}, bf16[256,1152]{1,0:T(8,128)(2,1)}) custom-call(s32[1]{0:T(128)} %bitcast.row_ref, bf16[256,2304]{1,0:T(8,128)(2,1)} %left_ref.1, bf16[256,2304]{1,0:T(8,128)(2,1)} %right_ref.1), custom_call_target="tpu_custom_call" | custom-call | bytes 4718592 | tf_op jit(solution)/shard_map/pallas_call | solution.py:72
  50.4 1.7 collective-permute-start.19
  52.1 1.6 select_select_fusion.7
  55.2 2.3 collective-permute-start.10
  59.6 2.7 collective-permute-done.10
  62.2 21.9 %collective-permute-done.9 = bf16[1,64,1024]{2,1,0:T(8,128)(2,1)S(1)} collective-permute-done((bf16[1,64,1024]{2,1,0:T(8,128)(2,1)S(1)}, bf16[1,64,1024]{2,1,0:T(8,128)(2,1)S(1)}, u32[]{:S(2)}, u32[]{:S(2)}) %collective-permute-start.9) | collective-permute-done | bytes 131104 | tf_op jit(solution)/shard_map/ppermute | solution.py:306
  85.3 1.8 collective-permute-start.14
  87.3 1.5 collective-permute-start.16
  88.8 3.0 collective-permute-done.14
  91.8 2.8 collective-permute-start.15
  94.6 2.8 collective-permute-done.15
  97.7 1.4 select_select_fusion.3
  102.0 2.1 multiply_convert_fusion.2
  104.1 1.6 fusion.1
  106.2 1.6 collective-permute-done.21
  108.1 2.6 collective-permute-start.24
  111.7 3.4 %collective-permute-done.24 = bf16[1,64,1024]{2,1,0:T(8,128)(2,1)S(1)} collective-permute-done((bf16[1,64,1024]{2,1,0:T(8,128)(2,1)S(1)}, bf16[1,64,1024]{2,1,0:T(8,128)(2,1)S(1)}, u32[]{:S(2)}, u32[]{:S(2)}) %collective-permute-start.24) | collective-permute-done | bytes 131104 | tf_op jit(solution)/shard_map/ppermute | solution.py:306
  115.1 2.5 collective-permute-done.23
  118.3 1.5 collective-permute-start.25
  119.8 1.7 collective-permute-start.27
  121.8 3.8 %collective-permute-done.25 = bf16[64,1024]{1,0:T(8,128)(2,1)S(1)} collective-permute-done((bf16[64,1024]{1,0:T(8,128)(2,1)S(1)}, bf16[64,1024]{1,0:T(8,128)(2,1)S(1)}, u32[]{:S(2)}, u32[]{:S(2)}) %collective-permute-start.25) | collective-permute-done | bytes 131104 | tf_op jit(solution)/shard_map/ppermute | solution.py:306
  125.6 1.5 collective-permute-done.27
  127.7 3.5 %collective-permute-start.48 = (bf16[64,1024]{1,0:T(8,128)(2,1)S(1)}, bf16[64,1024]{1,0:T(8,128)(2,1)S(1)}, u32[]{:S(2)}, u32[]{:S(2)}) collective-permute-start(bf16[64,1024]{1,0:T(8,128)(2,1)S(1)} %multiply_convert_fusion.3), channel_id=1, source_target_pairs={{0,24},{8,16},{16,8},{24,0},{1,25},{9,17},{17,9},{25,1},{2,26},{10... | collective-permute-start | bytes 393224 | tf_op jit(solution)/shard_map/ppermute | solution.py:299
  133.8 3.4 %collective-permute-start.55 = (bf16[2,256,256]{2,1,0:T(8,128)(2,1)}, bf16[2,256,256]{2,1,0:T(8,128)(2,1)S(1)}, u32[]{:S(2)}, u32[]{:S(2)}) collective-permute-start(bf16[2,256,256]{2,1,0:T(8,128)(2,1)} %pad_maximum_fusion.18), channel_id=1, source_target_pairs={{0,24},{8,16},{16,8},{24,0},{1,25},{9,17},{17,9},{25,1},{2,26},{10... | collective-permute-start | bytes 786440 | tf_op jit(solution)/shard_map/ppermute | solution.py:299
  137.3 4.9 %collective-permute-start.54 = (bf16[2,256,256]{2,1,0:T(8,128)(2,1)}, bf16[2,256,256]{2,1,0:T(8,128)(2,1)S(1)}, u32[]{:S(2)}, u32[]{:S(2)}) collective-permute-start(bf16[2,256,256]{2,1,0:T(8,128)(2,1)} %pad_maximum_fusion.18), channel_id=1, source_target_pairs={{0,16},{8,24},{16,0},{24,8},{1,17},{9,25},{17,1},{25,9},{2,18},{10... | collective-permute-start | bytes 786440 | tf_op jit(solution)/shard_map/ppermute | solution.py:299
  142.2 12.5 %collective-permute-done.47 = bf16[64,1024]{1,0:T(8,128)(2,1)S(1)} collective-permute-done((bf16[64,1024]{1,0:T(8,128)(2,1)S(1)}, bf16[64,1024]{1,0:T(8,128)(2,1)S(1)}, u32[]{:S(2)}, u32[]{:S(2)}) %collective-permute-start.47) | collective-permute-done | bytes 131104 | tf_op jit(solution)/shard_map/ppermute | solution.py:299
  154.8 1.7 collective-permute-start.49
  163.5 2.5 collective-permute-start.38
  168.6 5.7 %collective-permute-done.53 = bf16[2,256,256]{2,1,0:T(8,128)(2,1)} collective-permute-done((bf16[2,256,256]{2,1,0:T(8,128)(2,1)}, bf16[2,256,256]{2,1,0:T(8,128)(2,1)}, u32[]{:S(2)}, u32[]{:S(2)}) %collective-permute-start.53) | collective-permute-done | bytes 262176 | tf_op jit(solution)/shard_map/ppermute | solution.py:299
  176.5 4.3 %collective-permute-start.57 = (bf16[2,3,256,256]{3,2,1,0:T(8,128)(2,1)}, bf16[2,3,256,256]{3,2,1,0:T(8,128)(2,1)}, u32[]{:S(2)}, u32[]{:S(2)}) collective-permute-start(bf16[2,3,256,256]{3,2,1,0:T(8,128)(2,1)} %copy.58), channel_id=1, source_target_pairs={{0,1},{1,0},{2,3},{3,2},{4,5},{5,4},{6,7},{7,6},{8,9},{9,8},{10,11... | collective-permute-start | bytes 2359304 | tf_op jit(solution)/shard_map/ppermute | solution.py:306
  182.2 9.4 %collective-permute-done.37 = bf16[4,96,384]{2,1,0:T(8,128)(2,1)} collective-permute-done((bf16[4,96,384]{2,1,0:T(8,128)(2,1)}, bf16[4,96,384]{2,1,0:T(8,128)(2,1)}, u32[]{:S(2)}, u32[]{:S(2)}) %collective-permute-start.37) | collective-permute-done | bytes 294944 | tf_op jit(solution)/shard_map/ppermute | solution.py:299
  191.6 1.5 fusion.11
  195.8 1.9 collective-permute-done.41
  199.6 3.1 collective-permute-start.43
  202.7 10.4 %collective-permute-done.42.refs_1_ = bf16[4,96,384]{2,1,0:T(8,128)(2,1)S(1)} collective-permute-done((bf16[4,96,384]{2,1,0:T(8,128)(2,1)S(1)}, bf16[4,96,384]{2,1,0:T(8,128)(2,1)S(1)}, u32[]{:S(2)}, u32[]{:S(2)}) %collective-permute-start.42) | collective-permute-done | bytes 294944 | tf_op jit(solution)/shard_map/ppermute | solution.py:299
  215.2 2.5 pad_maximum_fusion
  217.7 6.6 %collective-permute-done.44.refs_3_ = bf16[4,96,384]{2,1,0:T(8,128)(2,1)S(1)} collective-permute-done((bf16[4,96,384]{2,1,0:T(8,128)(2,1)S(1)}, bf16[4,96,384]{2,1,0:T(8,128)(2,1)S(1)}, u32[]{:S(2)}, u32[]{:S(2)}) %collective-permute-start.44) | collective-permute-done | bytes 294944 | tf_op jit(solution)/shard_map/ppermute | solution.py:299
  225.0 3.1 shard_map.213
  229.6 3.4 %fusion = bf16[2,2,64,2048]{3,2,1,0:T(8,128)(2,1)} fusion(f32[2,2,2,64,2048]{4,3,2,1,0:T(8,128)} %bitcast.401, pred[]{:T(512)S(6)} %lt.79), kind=kLoop, calls=%fused_computation.23 | loop fusion | flops 524288 | bytes 3145729 | tf_op jit(solution)/shard_map/convert_element_type | solution.py:400
  236.1 3.1 collective-permute-done.56
  241.4 2.3 maximum_maximum_fusion
  244.8 1.6 copy-done.59
  246.4 11.8 %shard_map.214 = (bf16[1536,576]{1,0:T(8,128)(2,1)}, bf16[1536,1152]{1,0:T(8,128)(2,1)}) custom-call(bf16[1536,1024]{1,0:T(8,128)(2,1)} %bitcast.448, bf16[1536,1024]{1,0:T(8,128)(2,1)} %bitcast.416, bf16[1024,1152]{1,0:T(8,128)(2,1)} %copy-done.6, bf16[576,1024]{1,0:T(8,128)(2,1)} %copy-done.12), custom_call_target="tpu_custom_call" | custom-call | flops 5435817984 | bytes 15138816 | tf_op jit(solution)/shard_map/pallas_call | solution.py:105
  258.2 6.6 %fusion.78 = f32[1024,1152]{1,0:T(8,128)S(1)} fusion(bf16[1536,1024]{1,0:T(8,128)(2,1)S(1)} %bitcast.449, bf16[1536,1152]{1,0:T(8,128)(2,1)} %get-tuple-element.58), kind=kOutput, calls=%fused_computation.294 | convolution fusion | flops 3623878656 | bytes 11403264 | tf_op jit(solution)/shard_map/dot_general | solution.py:18
  264.9 1.6 convolution_add_fusion
  268.8 2.1 fusion.79
  274.0 1.8 bitcast_add_fusion
  276.0 1.7 collective-permute-start.32
  277.7 16.9 %collective-permute-done.64 = bf16[576,256]{1,0:T(8,128)(2,1)S(1)} collective-permute-done((bf16[576,256]{1,0:T(8,128)(2,1)S(1)}, bf16[576,256]{1,0:T(8,128)(2,1)S(1)}, u32[]{:S(2)}, u32[]{:S(2)}) %collective-permute-start.64) | collective-permute-done | bytes 294944 | tf_op jit(solution)/shard_map/ppermute | solution.py:294
  295.7 6.4 %collective-permute-done.63 = bf16[576,256]{1,0:T(8,128)(2,1)S(1)} collective-permute-done((bf16[576,256]{1,0:T(8,128)(2,1)S(1)}, bf16[576,256]{1,0:T(8,128)(2,1)S(1)}, u32[]{:S(2)}, u32[]{:S(2)}) %collective-permute-start.63) | collective-permute-done | bytes 294944 | tf_op jit(solution)/shard_map/ppermute | solution.py:294
  303.9 3.4 %collective-permute-done.31 = bf16[1,64,2048]{2,1,0:T(8,128)(2,1)S(1)} collective-permute-done((bf16[1,64,2048]{2,1,0:T(8,128)(2,1)S(1)}, bf16[1,64,2048]{2,1,0:T(8,128)(2,1)S(1)}, u32[]{:S(2)}, u32[]{:S(2)}) %collective-permute-start.31) | collective-permute-done | bytes 262176 | tf_op jit(solution)/shard_map/ppermute | solution.py:306
  307.3 1.9 collective-permute-done.30
  313.6 1.6 pad_maximum_fusion.2
  315.1 4.4 %collective-permute-done.61.refs_3_ = bf16[256,1152]{1,0:T(8,128)(2,1)S(1)} collective-permute-done((bf16[256,1152]{1,0:T(8,128)(2,1)S(1)}, bf16[256,1152]{1,0:T(8,128)(2,1)S(1)}, u32[]{:S(2)}, u32[]{:S(2)}) %collective-permute-start.61) | collective-permute-done | bytes 589856 | tf_op jit(solution)/shard_map/ppermute | solution.py:294
  320.3 4.2 %shard_map.215 = (f32[256,2304]{1,0:T(8,128)}, f32[256,2304]{1,0:T(8,128)}) custom-call(s32[1]{0:T(128)} %bitcast.row_ref, bf16[256,1152]{1,0:T(8,128)(2,1)} %get-tuple-element.81.refs_0_, bf16[256,1152]{1,0:T(8,128)(2,1)} %copy-done.23, bf16[256,1152]{1,0:T(8,128)(2,1)} %copy-done.24, bf16[256,1152]{1,0:T(8,128)(2,1)} %copy-done.25), custom_call_target="tpu_custom_call" | custom-call | bytes 7077888 | tf_op jit(solution)/shard_map/pallas_call | solution.py:194
  (354 shorter events, 76.0 us)
Async XLA Ops:
  2.4 12.5 %collective-permute-start.2 = (bf16[272,512]{1,0:T(8,128)(2,1)S(1)}, bf16[272,512]{1,0:T(8,128)(2,1)S(1)}, u32[]{:S(2)}, u32[]{:S(2)}) collective-permute-start(bf16[272,512]{1,0:T(8,128)(2,1)S(1)} %get-tuple-element.144), channel_id=1, source_target_pairs={{0,5},{1,4},{2,7},{3,6},{4,1},{5,0},{6,3},{7,2},{8,13},{9,12},{10,... | collective-permute-start | bytes 835592 | tf_op jit(solution)/shard_map/ppermute | solution.py:306
  6.4 12.9 %collective-permute-start.1 = (bf16[272,512]{1,0:T(8,128)(2,1)S(1)}, bf16[272,512]{1,0:T(8,128)(2,1)S(1)}, u32[]{:S(2)}, u32[]{:S(2)}) collective-permute-start(bf16[272,512]{1,0:T(8,128)(2,1)S(1)} %get-tuple-element.144), channel_id=1, source_target_pairs={{0,1},{1,0},{2,3},{3,2},{4,5},{5,4},{6,7},{7,6},{8,9},{9,8},{10,11... | collective-permute-start | bytes 835592 | tf_op jit(solution)/shard_map/ppermute | solution.py:306
  6.9 12.4 %collective-permute-start = (bf16[272,512]{1,0:T(8,128)(2,1)S(1)}, bf16[272,512]{1,0:T(8,128)(2,1)S(1)}, u32[]{:S(2)}, u32[]{:S(2)}) collective-permute-start(bf16[272,512]{1,0:T(8,128)(2,1)S(1)} %get-tuple-element.144), channel_id=1, source_target_pairs={{0,4},{1,5},{2,6},{3,7},{4,0},{5,1},{6,2},{7,3},{8,12},{9,13},{10,... | collective-permute-start | bytes 835592 | tf_op jit(solution)/shard_map/ppermute | solution.py:306
  11.5 13.8 %collective-permute-start.6 = (bf16[384,384]{1,0:T(8,128)(2,1)}, bf16[384,384]{1,0:T(8,128)(2,1)}, u32[]{:S(2)}, u32[]{:S(2)}) collective-permute-start(bf16[384,384]{1,0:T(8,128)(2,1)} %fusion.26), channel_id=1, source_target_pairs={{0,6},{2,4},{4,2},{6,0},{1,7},{3,5},{5,3},{7,1},{8,14},{10,12},{12... | collective-permute-start | bytes 884744 | tf_op jit(solution)/shard_map/ppermute | solution.py:294
  12.8 19.1 %collective-permute-start.5 = (bf16[384,384]{1,0:T(8,128)(2,1)}, bf16[384,384]{1,0:T(8,128)(2,1)}, u32[]{:S(2)}, u32[]{:S(2)}) collective-permute-start(bf16[384,384]{1,0:T(8,128)(2,1)} %fusion.25), channel_id=1, source_target_pairs={{0,4},{2,6},{4,0},{6,2},{1,5},{3,7},{5,1},{7,3},{8,12},{10,14},{12... | collective-permute-start | bytes 884744 | tf_op jit(solution)/shard_map/ppermute | solution.py:294
  14.9 16.9 %collective-permute-start.4 = (bf16[384,384]{1,0:T(8,128)(2,1)}, bf16[384,384]{1,0:T(8,128)(2,1)}, u32[]{:S(2)}, u32[]{:S(2)}) collective-permute-start(bf16[384,384]{1,0:T(8,128)(2,1)} %fusion.24), channel_id=1, source_target_pairs={{0,2},{2,0},{4,6},{6,4},{1,3},{3,1},{5,7},{7,5},{8,10},{10,8},{12,... | collective-permute-start | bytes 884744 | tf_op jit(solution)/shard_map/ppermute | solution.py:294
  20.2 16.2 %collective-permute-start.3 = (bf16[4,272,512]{2,1,0:T(8,128)(2,1)S(1)}, bf16[4,272,512]{2,1,0:T(8,128)(2,1)S(1)}, u32[]{:S(2)}, u32[]{:S(2)}) collective-permute-start(bf16[4,272,512]{2,1,0:T(8,128)(2,1)S(1)} %pad_maximum_fusion.5.own_ref), channel_id=1, source_target_pairs={{0,2},{1,3},{2,0},{3,1},{4,6},{5,7},{6,4},{7,5},{8,10},{9,11},{10,... | collective-permute-start | bytes 3342344 | tf_op jit(solution)/shard_map/ppermute | solution.py:306
  21.4 30.7 %collective-permute-start.12 = (bf16[576,256]{1,0:T(8,128)(2,1)}, bf16[576,256]{1,0:T(8,128)(2,1)}, u32[]{:S(2)}, u32[]{:S(2)}) collective-permute-start(bf16[576,256]{1,0:T(8,128)(2,1)} %get-tuple-element.110), channel_id=1, source_target_pairs={{0,4},{2,6},{4,0},{6,2},{1,5},{3,7},{5,1},{7,3},{8,12},{10,14},{12... | collective-permute-start | bytes 884744 | tf_op jit(solution)/shard_map/ppermute | solution.py:294
  25.3 26.7 %collective-permute-start.13 = (bf16[576,256]{1,0:T(8,128)(2,1)}, bf16[576,256]{1,0:T(8,128)(2,1)}, u32[]{:S(2)}, u32[]{:S(2)}) collective-permute-start(bf16[576,256]{1,0:T(8,128)(2,1)} %get-tuple-element.112), channel_id=1, source_target_pairs={{0,6},{2,4},{4,2},{6,0},{1,7},{3,5},{5,3},{7,1},{8,14},{10,12},{12... | collective-permute-start | bytes 884744 | tf_op jit(solution)/shard_map/ppermute | solution.py:294
  31.9 20.2 %collective-permute-start.11 = (bf16[576,256]{1,0:T(8,128)(2,1)}, bf16[576,256]{1,0:T(8,128)(2,1)}, u32[]{:S(2)}, u32[]{:S(2)}) collective-permute-start(bf16[576,256]{1,0:T(8,128)(2,1)} %get-tuple-element.111), channel_id=1, source_target_pairs={{0,2},{2,0},{4,6},{6,4},{1,3},{3,1},{5,7},{7,5},{8,10},{10,8},{12,... | collective-permute-start | bytes 884744 | tf_op jit(solution)/shard_map/ppermute | solution.py:294
  46.0 7.7 %collective-permute-start.7 = (bf16[2,2,64,1024]{3,2,1,0:T(8,128)(2,1)}, bf16[2,2,64,1024]{3,2,1,0:T(8,128)(2,1)}, u32[]{:S(2)}, u32[]{:S(2)}) collective-permute-start(bf16[2,2,64,1024]{3,2,1,0:T(8,128)(2,1)} %fusion.12), channel_id=1, source_target_pairs={{0,2},{1,3},{2,0},{3,1},{4,6},{5,7},{6,4},{7,5},{8,10},{9,11},{10,... | collective-permute-start | bytes 1572872 | tf_op jit(solution)/shard_map/ppermute | solution.py:306
  50.4 47.2 %collective-permute-start.19 = (bf16[256,1152]{1,0:T(8,128)(2,1)}, bf16[256,1152]{1,0:T(8,128)(2,1)}, u32[]{:S(2)}, u32[]{:S(2)}) collective-permute-start(bf16[256,1152]{1,0:T(8,128)(2,1)} %get-tuple-element.43), channel_id=1, source_target_pairs={{0,4},{2,6},{4,0},{6,2},{1,5},{3,7},{5,1},{7,3},{8,12},{10,14},{12... | collective-permute-start | bytes 1769480 | tf_op jit(solution)/shard_map/ppermute | solution.py:294
  52.1 45.6 %collective-permute-start.20 = (bf16[256,1152]{1,0:T(8,128)(2,1)}, bf16[256,1152]{1,0:T(8,128)(2,1)S(1)}, u32[]{:S(2)}, u32[]{:S(2)}) collective-permute-start(bf16[256,1152]{1,0:T(8,128)(2,1)} %get-tuple-element.44), channel_id=1, source_target_pairs={{0,6},{2,4},{4,2},{6,0},{1,7},{3,5},{5,3},{7,1},{8,14},{10,12},{12... | collective-permute-start | bytes 1769480 | tf_op jit(solution)/shard_map/ppermute | solution.py:294
  55.2 7.1 %collective-permute-start.10 = (bf16[1,64,1024]{2,1,0:T(8,128)(2,1)S(1)}, bf16[1,64,1024]{2,1,0:T(8,128)(2,1)S(1)}, u32[]{:S(2)}, u32[]{:S(2)}) collective-permute-start(bf16[1,64,1024]{2,1,0:T(8,128)(2,1)S(1)} %get-tuple-element.127), channel_id=1, source_target_pairs={{0,5},{1,4},{2,7},{3,6},{4,1},{5,0},{6,3},{7,2},{8,13},{9,12},{10,... | collective-permute-start | bytes 393224 | tf_op jit(solution)/shard_map/ppermute | solution.py:306
  57.5 26.6 %collective-permute-start.9 = (bf16[1,64,1024]{2,1,0:T(8,128)(2,1)S(1)}, bf16[1,64,1024]{2,1,0:T(8,128)(2,1)S(1)}, u32[]{:S(2)}, u32[]{:S(2)}) collective-permute-start(bf16[1,64,1024]{2,1,0:T(8,128)(2,1)S(1)} %get-tuple-element.128), channel_id=1, source_target_pairs={{0,4},{1,5},{2,6},{3,7},{4,0},{5,1},{6,2},{7,3},{8,12},{9,13},{10,... | collective-permute-start | bytes 393224 | tf_op jit(solution)/shard_map/ppermute | solution.py:306
  58.2 25.9 %collective-permute-start.8 = (bf16[1,64,1024]{2,1,0:T(8,128)(2,1)S(1)}, bf16[1,64,1024]{2,1,0:T(8,128)(2,1)S(1)}, u32[]{:S(2)}, u32[]{:S(2)}) collective-permute-start(bf16[1,64,1024]{2,1,0:T(8,128)(2,1)S(1)} %get-tuple-element.126), channel_id=1, source_target_pairs={{0,1},{1,0},{2,3},{3,2},{4,5},{5,4},{6,7},{7,6},{8,9},{9,8},{10,11... | collective-permute-start | bytes 393224 | tf_op jit(solution)/shard_map/ppermute | solution.py:306
  62.2 35.4 %collective-permute-start.18 = (bf16[256,1152]{1,0:T(8,128)(2,1)S(1)}, bf16[256,1152]{1,0:T(8,128)(2,1)S(1)}, u32[]{:S(2)}, u32[]{:S(2)}) collective-permute-start(bf16[256,1152]{1,0:T(8,128)(2,1)S(1)} %copy-done.73), channel_id=1, source_target_pairs={{0,2},{2,0},{4,6},{6,4},{1,3},{3,1},{5,7},{7,5},{8,10},{10,8},{12,... | collective-permute-start | bytes 1769480 | tf_op jit(solution)/shard_map/ppermute | solution.py:294
  85.3 6.4 %collective-permute-start.14 = (bf16[64,1024]{1,0:T(8,128)(2,1)S(1)}, bf16[64,1024]{1,0:T(8,128)(2,1)S(1)}, u32[]{:S(2)}, u32[]{:S(2)}) collective-permute-start(bf16[64,1024]{1,0:T(8,128)(2,1)S(1)} %multiply_convert_fusion.3), channel_id=1, source_target_pairs={{0,4},{1,5},{2,6},{3,7},{4,0},{5,1},{6,2},{7,3},{8,12},{9,13},{10,... | collective-permute-start | bytes 393224 | tf_op jit(solution)/shard_map/ppermute | solution.py:306
  87.3 7.4 %collective-permute-start.16 = (bf16[64,1024]{1,0:T(8,128)(2,1)S(1)}, bf16[64,1024]{1,0:T(8,128)(2,1)S(1)}, u32[]{:S(2)}, u32[]{:S(2)}) collective-permute-start(bf16[64,1024]{1,0:T(8,128)(2,1)S(1)} %multiply_convert_fusion.3), channel_id=1, source_target_pairs={{0,5},{1,4},{2,7},{3,6},{4,1},{5,0},{6,3},{7,2},{8,13},{9,12},{10,... | collective-permute-start | bytes 393224 | tf_op jit(solution)/shard_map/ppermute | solution.py:306
  91.8 5.7 %collective-permute-start.15 = (bf16[64,1024]{1,0:T(8,128)(2,1)S(1)}, bf16[64,1024]{1,0:T(8,128)(2,1)S(1)}, u32[]{:S(2)}, u32[]{:S(2)}) collective-permute-start(bf16[64,1024]{1,0:T(8,128)(2,1)S(1)} %multiply_convert_fusion.3), channel_id=1, source_target_pairs={{0,1},{1,0},{2,3},{3,2},{4,5},{5,4},{6,7},{7,6},{8,9},{9,8},{10,11... | collective-permute-start | bytes 393224 | tf_op jit(solution)/shard_map/ppermute | solution.py:306
  97.6 2.0 collective-permute-start.17
  108.1 7.0 %collective-permute-start.24 = (bf16[1,64,1024]{2,1,0:T(8,128)(2,1)S(1)}, bf16[1,64,1024]{2,1,0:T(8,128)(2,1)S(1)}, u32[]{:S(2)}, u32[]{:S(2)}) collective-permute-start(bf16[1,64,1024]{2,1,0:T(8,128)(2,1)S(1)} %get-tuple-element.124), channel_id=1, source_target_pairs={{0,5},{1,4},{2,7},{3,6},{4,1},{5,0},{6,3},{7,2},{8,13},{9,12},{10,... | collective-permute-start | bytes 393224 | tf_op jit(solution)/shard_map/ppermute | solution.py:306
  110.7 6.9 %collective-permute-start.23 = (bf16[1,64,1024]{2,1,0:T(8,128)(2,1)S(1)}, bf16[1,64,1024]{2,1,0:T(8,128)(2,1)S(1)}, u32[]{:S(2)}, u32[]{:S(2)}) collective-permute-start(bf16[1,64,1024]{2,1,0:T(8,128)(2,1)S(1)} %get-tuple-element.125), channel_id=1, source_target_pairs={{0,4},{1,5},{2,6},{3,7},{4,0},{5,1},{6,2},{7,3},{8,12},{9,13},{10,... | collective-permute-start | bytes 393224 | tf_op jit(solution)/shard_map/ppermute | solution.py:306
  111.7 6.2 %collective-permute-start.22 = (bf16[1,64,1024]{2,1,0:T(8,128)(2,1)S(1)}, bf16[1,64,1024]{2,1,0:T(8,128)(2,1)S(1)}, u32[]{:S(2)}, u32[]{:S(2)}) collective-permute-start(bf16[1,64,1024]{2,1,0:T(8,128)(2,1)S(1)} %get-tuple-element.123), channel_id=1, source_target_pairs={{0,1},{1,0},{2,3},{3,2},{4,5},{5,4},{6,7},{7,6},{8,9},{9,8},{10,11... | collective-permute-start | bytes 393224 | tf_op jit(solution)/shard_map/ppermute | solution.py:306
  118.3 7.3 %collective-permute-start.25 = (bf16[64,1024]{1,0:T(8,128)(2,1)S(1)}, bf16[64,1024]{1,0:T(8,128)(2,1)S(1)}, u32[]{:S(2)}, u32[]{:S(2)}) collective-permute-start(bf16[64,1024]{1,0:T(8,128)(2,1)S(1)} %fusion.67), channel_id=1, source_target_pairs={{0,4},{1,5},{2,6},{3,7},{4,0},{5,1},{6,2},{7,3},{8,12},{9,13},{10,... | collective-permute-start | bytes 393224 | tf_op jit(solution)/shard_map/ppermute | solution.py:306
  119.8 7.3 %collective-permute-start.27 = (bf16[64,1024]{1,0:T(8,128)(2,1)S(1)}, bf16[64,1024]{1,0:T(8,128)(2,1)S(1)}, u32[]{:S(2)}, u32[]{:S(2)}) collective-permute-start(bf16[64,1024]{1,0:T(8,128)(2,1)S(1)} %fusion.67), channel_id=1, source_target_pairs={{0,5},{1,4},{2,7},{3,6},{4,1},{5,0},{6,3},{7,2},{8,13},{9,12},{10,... | collective-permute-start | bytes 393224 | tf_op jit(solution)/shard_map/ppermute | solution.py:306
  121.5 6.1 %collective-permute-start.26 = (bf16[64,1024]{1,0:T(8,128)(2,1)S(1)}, bf16[64,1024]{1,0:T(8,128)(2,1)S(1)}, u32[]{:S(2)}, u32[]{:S(2)}) collective-permute-start(bf16[64,1024]{1,0:T(8,128)(2,1)S(1)} %fusion.67), channel_id=1, source_target_pairs={{0,1},{1,0},{2,3},{3,2},{4,5},{5,4},{6,7},{7,6},{8,9},{9,8},{10,11... | collective-permute-start | bytes 393224 | tf_op jit(solution)/shard_map/ppermute | solution.py:306
  127.6 28.8 %collective-permute-start.28 = (bf16[4,64,1024]{2,1,0:T(8,128)(2,1)S(1)}, bf16[4,64,1024]{2,1,0:T(8,128)(2,1)S(1)}, u32[]{:S(2)}, u32[]{:S(2)}) collective-permute-start(bf16[4,64,1024]{2,1,0:T(8,128)(2,1)S(1)} %pad_maximum_fusion.12), channel_id=1, source_target_pairs={{0,2},{1,3},{2,0},{3,1},{4,6},{5,7},{6,4},{7,5},{8,10},{9,11},{10,... | collective-permute-start | bytes 1572872 | tf_op jit(solution)/shard_map/ppermute | solution.py:306
  127.7 9.6 %collective-permute-start.48 = (bf16[64,1024]{1,0:T(8,128)(2,1)S(1)}, bf16[64,1024]{1,0:T(8,128)(2,1)S(1)}, u32[]{:S(2)}, u32[]{:S(2)}) collective-permute-start(bf16[64,1024]{1,0:T(8,128)(2,1)S(1)} %multiply_convert_fusion.3), channel_id=1, source_target_pairs={{0,24},{8,16},{16,8},{24,0},{1,25},{9,17},{17,9},{25,1},{2,26},{10... | collective-permute-start | bytes 393224 | tf_op jit(solution)/shard_map/ppermute | solution.py:299
  131.2 23.4 %collective-permute-start.47 = (bf16[64,1024]{1,0:T(8,128)(2,1)S(1)}, bf16[64,1024]{1,0:T(8,128)(2,1)S(1)}, u32[]{:S(2)}, u32[]{:S(2)}) collective-permute-start(bf16[64,1024]{1,0:T(8,128)(2,1)S(1)} %multiply_convert_fusion.3), channel_id=1, source_target_pairs={{0,16},{8,24},{16,0},{24,8},{1,17},{9,25},{17,1},{25,9},{2,18},{10... | collective-permute-start | bytes 393224 | tf_op jit(solution)/shard_map/ppermute | solution.py:299
  131.3 23.4 %collective-permute-start.46 = (bf16[64,1024]{1,0:T(8,128)(2,1)S(1)}, bf16[64,1024]{1,0:T(8,128)(2,1)S(1)}, u32[]{:S(2)}, u32[]{:S(2)}) collective-permute-start(bf16[64,1024]{1,0:T(8,128)(2,1)S(1)} %multiply_convert_fusion.3), channel_id=1, source_target_pairs={{0,8},{8,0},{16,24},{24,16},{1,9},{9,1},{17,25},{25,17},{2,10},{10... | collective-permute-start | bytes 393224 | tf_op jit(solution)/shard_map/ppermute | solution.py:299
  133.8 32.1 %collective-permute-start.55 = (bf16[2,256,256]{2,1,0:T(8,128)(2,1)}, bf16[2,256,256]{2,1,0:T(8,128)(2,1)S(1)}, u32[]{:S(2)}, u32[]{:S(2)}) collective-permute-start(bf16[2,256,256]{2,1,0:T(8,128)(2,1)} %pad_maximum_fusion.18), channel_id=1, source_target_pairs={{0,24},{8,16},{16,8},{24,0},{1,25},{9,17},{17,9},{25,1},{2,26},{10... | collective-permute-start | bytes 786440 | tf_op jit(solution)/shard_map/ppermute | solution.py:299
  137.3 29.7 %collective-permute-start.54 = (bf16[2,256,256]{2,1,0:T(8,128)(2,1)}, bf16[2,256,256]{2,1,0:T(8,128)(2,1)S(1)}, u32[]{:S(2)}, u32[]{:S(2)}) collective-permute-start(bf16[2,256,256]{2,1,0:T(8,128)(2,1)} %pad_maximum_fusion.18), channel_id=1, source_target_pairs={{0,16},{8,24},{16,0},{24,8},{1,17},{9,25},{17,1},{25,9},{2,18},{10... | collective-permute-start | bytes 786440 | tf_op jit(solution)/shard_map/ppermute | solution.py:299
  154.7 19.6 %collective-permute-start.53 = (bf16[2,256,256]{2,1,0:T(8,128)(2,1)}, bf16[2,256,256]{2,1,0:T(8,128)(2,1)}, u32[]{:S(2)}, u32[]{:S(2)}) collective-permute-start(bf16[2,256,256]{2,1,0:T(8,128)(2,1)} %pad_maximum_fusion.18), channel_id=1, source_target_pairs={{0,8},{8,0},{16,24},{24,16},{1,9},{9,1},{17,25},{25,17},{2,10},{10... | collective-permute-start | bytes 786440 | tf_op jit(solution)/shard_map/ppermute | solution.py:299
  154.8 26.1 %collective-permute-start.49 = (bf16[1,3,64,1024]{3,2,1,0:T(8,128)(2,1)S(1)}, bf16[1,3,64,1024]{3,2,1,0:T(8,128)(2,1)}, u32[]{:S(2)}, u32[]{:S(2)}) collective-permute-start(bf16[1,3,64,1024]{3,2,1,0:T(8,128)(2,1)S(1)} %maximum_bitcast_fusion), channel_id=1, source_target_pairs={{0,4},{1,5},{2,6},{3,7},{4,0},{5,1},{6,2},{7,3},{8,12},{9,13},{10,... | collective-permute-start | bytes 1179656 | tf_op jit(solution)/shard_map/ppermute | solution.py:306
  163.5 18.6 %collective-permute-start.38 = (bf16[4,96,384]{2,1,0:T(8,128)(2,1)}, bf16[4,96,384]{2,1,0:T(8,128)(2,1)}, u32[]{:S(2)}, u32[]{:S(2)}) collective-permute-start(bf16[4,96,384]{2,1,0:T(8,128)(2,1)} %get-tuple-element.87), channel_id=1, source_target_pairs={{0,24},{8,16},{16,8},{24,0},{1,25},{9,17},{17,9},{25,1},{2,26},{10... | collective-permute-start | bytes 884744 | tf_op jit(solution)/shard_map/ppermute | solution.py:299
  166.0 25.6 %collective-permute-start.37 = (bf16[4,96,384]{2,1,0:T(8,128)(2,1)}, bf16[4,96,384]{2,1,0:T(8,128)(2,1)}, u32[]{:S(2)}, u32[]{:S(2)}) collective-permute-start(bf16[4,96,384]{2,1,0:T(8,128)(2,1)} %get-tuple-element.86), channel_id=1, source_target_pairs={{0,16},{8,24},{16,0},{24,8},{1,17},{9,25},{17,1},{25,9},{2,18},{10... | collective-permute-start | bytes 884744 | tf_op jit(solution)/shard_map/ppermute | solution.py:299
  167.7 23.9 %collective-permute-start.36 = (bf16[4,96,384]{2,1,0:T(8,128)(2,1)S(1)}, bf16[4,96,384]{2,1,0:T(8,128)(2,1)}, u32[]{:S(2)}, u32[]{:S(2)}) collective-permute-start(bf16[4,96,384]{2,1,0:T(8,128)(2,1)S(1)} %get-tuple-element.85), channel_id=1, source_target_pairs={{0,8},{8,0},{16,24},{24,16},{1,9},{9,1},{17,25},{25,17},{2,10},{10... | collective-permute-start | bytes 884744 | tf_op jit(solution)/shard_map/ppermute | solution.py:299
  176.5 56.9 %collective-permute-start.57 = (bf16[2,3,256,256]{3,2,1,0:T(8,128)(2,1)}, bf16[2,3,256,256]{3,2,1,0:T(8,128)(2,1)}, u32[]{:S(2)}, u32[]{:S(2)}) collective-permute-start(bf16[2,3,256,256]{3,2,1,0:T(8,128)(2,1)} %copy.58), channel_id=1, source_target_pairs={{0,1},{1,0},{2,3},{3,2},{4,5},{5,4},{6,7},{7,6},{8,9},{9,8},{10,11... | collective-permute-start | bytes 2359304 | tf_op jit(solution)/shard_map/ppermute | solution.py:306
  181.9 51.1 %collective-permute-start.51 = (bf16[2,3,64,1024]{3,2,1,0:T(8,128)(2,1)S(1)}, bf16[2,3,64,1024]{3,2,1,0:T(8,128)(2,1)S(1)}, u32[]{:S(2)}, u32[]{:S(2)}) collective-permute-start(bf16[2,3,64,1024]{3,2,1,0:T(8,128)(2,1)S(1)} %pad_maximum_fusion.7), channel_id=1, source_target_pairs={{0,1},{1,0},{2,3},{3,2},{4,5},{5,4},{6,7},{7,6},{8,9},{9,8},{10,11... | collective-permute-start | bytes 2359304 | tf_op jit(solution)/shard_map/ppermute | solution.py:306
  193.1 4.6 %collective-permute-start.41 = (bf16[96,384]{1,0:T(8,128)(2,1)S(1)}, bf16[96,384]{1,0:T(8,128)(2,1)S(1)}, u32[]{:S(2)}, u32[]{:S(2)}) collective-permute-start(bf16[96,384]{1,0:T(8,128)(2,1)S(1)} %get-tuple-element.140), channel_id=1, source_target_pairs={{0,6},{2,4},{4,2},{6,0},{1,7},{3,5},{5,3},{7,1},{8,14},{10,12},{12... | collective-permute-start | bytes 221192 | tf_op jit(solution)/shard_map/ppermute | solution.py:294
  193.3 5.2 %collective-permute-start.40 = (bf16[96,384]{1,0:T(8,128)(2,1)S(1)}, bf16[96,384]{1,0:T(8,128)(2,1)S(1)}, u32[]{:S(2)}, u32[]{:S(2)}) collective-permute-start(bf16[96,384]{1,0:T(8,128)(2,1)S(1)} %get-tuple-element.141), channel_id=1, source_target_pairs={{0,4},{2,6},{4,0},{6,2},{1,5},{3,7},{5,1},{7,3},{8,12},{10,14},{12... | collective-permute-start | bytes 221192 | tf_op jit(solution)/shard_map/ppermute | solution.py:294
  194.2 4.3 %collective-permute-start.39 = (bf16[96,384]{1,0:T(8,128)(2,1)S(1)}, bf16[96,384]{1,0:T(8,128)(2,1)S(1)}, u32[]{:S(2)}, u32[]{:S(2)}) collective-permute-start(bf16[96,384]{1,0:T(8,128)(2,1)S(1)} %get-tuple-element.142), channel_id=1, source_target_pairs={{0,2},{2,0},{4,6},{6,4},{1,3},{3,1},{5,7},{7,5},{8,10},{10,8},{12,... | collective-permute-start | bytes 221192 | tf_op jit(solution)/shard_map/ppermute | solution.py:294
  197.7 37.5 %collective-permute-start.50 = (bf16[2,3,64,1024]{3,2,1,0:T(8,128)(2,1)S(1)}, bf16[2,3,64,1024]{3,2,1,0:T(8,128)(2,1)S(1)}, u32[]{:S(2)}, u32[]{:S(2)}) collective-permute-start(bf16[2,3,64,1024]{3,2,1,0:T(8,128)(2,1)S(1)} %pad_maximum_fusion.7), channel_id=1, source_target_pairs={{0,2},{1,3},{2,0},{3,1},{4,6},{5,7},{6,4},{7,5},{8,10},{9,11},{10,... | collective-permute-start | bytes 2359304 | tf_op jit(solution)/shard_map/ppermute | solution.py:306
  198.5 14.6 %collective-permute-start.42 = (bf16[4,96,384]{2,1,0:T(8,128)(2,1)S(1)}, bf16[4,96,384]{2,1,0:T(8,128)(2,1)S(1)}, u32[]{:S(2)}, u32[]{:S(2)}) collective-permute-start(bf16[4,96,384]{2,1,0:T(8,128)(2,1)S(1)} %pad_maximum_fusion.15.refs_0_), channel_id=1, source_target_pairs={{0,8},{8,0},{16,24},{24,16},{1,9},{9,1},{17,25},{25,17},{2,10},{10... | collective-permute-start | bytes 884744 | tf_op jit(solution)/shard_map/ppermute | solution.py:299
  199.6 18.1 %collective-permute-start.43 = (bf16[4,96,384]{2,1,0:T(8,128)(2,1)S(1)}, bf16[4,96,384]{2,1,0:T(8,128)(2,1)S(1)}, u32[]{:S(2)}, u32[]{:S(2)}) collective-permute-start(bf16[4,96,384]{2,1,0:T(8,128)(2,1)S(1)} %pad_maximum_fusion.15.refs_0_), channel_id=1, source_target_pairs={{0,16},{8,24},{16,0},{24,8},{1,17},{9,25},{17,1},{25,9},{2,18},{10... | collective-permute-start | bytes 884744 | tf_op jit(solution)/shard_map/ppermute | solution.py:299
  213.8 10.5 %collective-permute-start.44 = (bf16[4,96,384]{2,1,0:T(8,128)(2,1)S(1)}, bf16[4,96,384]{2,1,0:T(8,128)(2,1)S(1)}, u32[]{:S(2)}, u32[]{:S(2)}) collective-permute-start(bf16[4,96,384]{2,1,0:T(8,128)(2,1)S(1)} %pad_maximum_fusion.15.refs_0_), channel_id=1, source_target_pairs={{0,24},{8,16},{16,8},{24,0},{1,25},{9,17},{17,9},{25,1},{2,26},{10... | collective-permute-start | bytes 884744 | tf_op jit(solution)/shard_map/ppermute | solution.py:299
  228.9 5.4 %collective-permute-start.45 = (f32[2,256]{1,0:T(2,128)S(1)}, f32[2,256]{1,0:T(2,128)S(1)}, u32[]{:S(2)}, u32[]{:S(2)}) collective-permute-start(f32[2,256]{1,0:T(2,128)S(1)} %reshape.555), channel_id=1, source_target_pairs={{0,1},{1,0},{2,3},{3,2},{4,5},{5,4},{6,7},{7,6},{8,9},{9,8},{10,11... | collective-permute-start | bytes 6152 | tf_op jit(solution)/shard_map/ppermute | solution.py:637
  232.9 40.0 %collective-permute-start.29 = (bf16[2,2,64,2048]{3,2,1,0:T(8,128)(2,1)}, bf16[2,2,64,2048]{3,2,1,0:T(8,128)(2,1)}, u32[]{:S(2)}, u32[]{:S(2)}) collective-permute-start(bf16[2,2,64,2048]{3,2,1,0:T(8,128)(2,1)} %fusion), channel_id=1, source_target_pairs={{0,2},{1,3},{2,0},{3,1},{4,6},{5,7},{6,4},{7,5},{8,10},{9,11},{10,... | collective-permute-start | bytes 3145736 | tf_op jit(solution)/shard_map/ppermute | solution.py:306
  233.0 10.8 %collective-permute-start.52 = (bf16[2,3,64,1024]{3,2,1,0:T(8,128)(2,1)S(1)}, bf16[2,3,64,1024]{3,2,1,0:T(8,128)(2,1)S(1)}, u32[]{:S(2)}, u32[]{:S(2)}) collective-permute-start(bf16[2,3,64,1024]{3,2,1,0:T(8,128)(2,1)S(1)} %collective-permute-done.51), channel_id=1, source_target_pairs={{0,2},{1,3},{2,0},{3,1},{4,6},{5,7},{6,4},{7,5},{8,10},{9,11},{10,... | collective-permute-start | bytes 2359304 | tf_op jit(solution)/shard_map/ppermute | solution.py:306
  233.5 6.3 %collective-permute-start.58 = (bf16[2,3,256,256]{3,2,1,0:T(8,128)(2,1)}, bf16[2,3,256,256]{3,2,1,0:T(8,128)(2,1)S(1)}, u32[]{:S(2)}, u32[]{:S(2)}) collective-permute-start(bf16[2,3,256,256]{3,2,1,0:T(8,128)(2,1)} %collective-permute-done.57), channel_id=1, source_target_pairs={{0,2},{1,3},{2,0},{3,1},{4,6},{5,7},{6,4},{7,5},{8,10},{9,11},{10,... | collective-permute-start | bytes 2359304 | tf_op jit(solution)/shard_map/ppermute | solution.py:306
  234.2 5.0 %collective-permute-start.56 = (bf16[2,3,256,256]{3,2,1,0:T(8,128)(2,1)S(1)}, bf16[2,3,256,256]{3,2,1,0:T(8,128)(2,1)S(1)}, u32[]{:S(2)}, u32[]{:S(2)}) collective-permute-start(bf16[2,3,256,256]{3,2,1,0:T(8,128)(2,1)S(1)} %copy.49), channel_id=1, source_target_pairs={{0,2},{1,3},{2,0},{3,1},{4,6},{5,7},{6,4},{7,5},{8,10},{9,11},{10,... | collective-permute-start | bytes 2359304 | tf_op jit(solution)/shard_map/ppermute | solution.py:306
  267.5 45.5 %collective-permute-start.59 = (bf16[256,1152]{1,0:T(8,128)(2,1)S(1)}, bf16[256,1152]{1,0:T(8,128)(2,1)S(1)}, u32[]{:S(2)}, u32[]{:S(2)}) collective-permute-start(bf16[256,1152]{1,0:T(8,128)(2,1)S(1)} %get-tuple-element.80), channel_id=1, source_target_pairs={{0,2},{2,0},{4,6},{6,4},{1,3},{3,1},{5,7},{7,5},{8,10},{10,8},{12,... | collective-permute-start | bytes 1769480 | tf_op jit(solution)/shard_map/ppermute | solution.py:294
  267.6 47.5 %collective-permute-start.60 = (bf16[256,1152]{1,0:T(8,128)(2,1)S(1)}, bf16[256,1152]{1,0:T(8,128)(2,1)S(1)}, u32[]{:S(2)}, u32[]{:S(2)}) collective-permute-start(bf16[256,1152]{1,0:T(8,128)(2,1)S(1)} %get-tuple-element.79), channel_id=1, source_target_pairs={{0,4},{2,6},{4,0},{6,2},{1,5},{3,7},{5,1},{7,3},{8,12},{10,14},{12... | collective-permute-start | bytes 1769480 | tf_op jit(solution)/shard_map/ppermute | solution.py:294
  271.8 4.2 %collective-permute-start.62 = (bf16[576,256]{1,0:T(8,128)(2,1)S(1)}, bf16[576,256]{1,0:T(8,128)(2,1)S(1)}, u32[]{:S(2)}, u32[]{:S(2)}) collective-permute-start(bf16[576,256]{1,0:T(8,128)(2,1)S(1)} %get-tuple-element.109), channel_id=1, source_target_pairs={{0,2},{2,0},{4,6},{6,4},{1,3},{3,1},{5,7},{7,5},{8,10},{10,8},{12,... | collective-permute-start | bytes 884744 | tf_op jit(solution)/shard_map/ppermute | solution.py:294
  271.9 22.6 %collective-permute-start.64 = (bf16[576,256]{1,0:T(8,128)(2,1)S(1)}, bf16[576,256]{1,0:T(8,128)(2,1)S(1)}, u32[]{:S(2)}, u32[]{:S(2)}) collective-permute-start(bf16[576,256]{1,0:T(8,128)(2,1)S(1)} %get-tuple-element.108), channel_id=1, source_target_pairs={{0,6},{2,4},{4,2},{6,0},{1,7},{3,5},{5,3},{7,1},{8,14},{10,12},{12... | collective-permute-start | bytes 884744 | tf_op jit(solution)/shard_map/ppermute | solution.py:294
  272.9 29.2 %collective-permute-start.63 = (bf16[576,256]{1,0:T(8,128)(2,1)S(1)}, bf16[576,256]{1,0:T(8,128)(2,1)S(1)}, u32[]{:S(2)}, u32[]{:S(2)}) collective-permute-start(bf16[576,256]{1,0:T(8,128)(2,1)S(1)} %get-tuple-element.107), channel_id=1, source_target_pairs={{0,4},{2,6},{4,0},{6,2},{1,5},{3,7},{5,1},{7,3},{8,12},{10,14},{12... | collective-permute-start | bytes 884744 | tf_op jit(solution)/shard_map/ppermute | solution.py:294
  276.0 27.9 %collective-permute-start.32 = (bf16[1,64,2048]{2,1,0:T(8,128)(2,1)S(1)}, bf16[1,64,2048]{2,1,0:T(8,128)(2,1)S(1)}, u32[]{:S(2)}, u32[]{:S(2)}) collective-permute-start(bf16[1,64,2048]{2,1,0:T(8,128)(2,1)S(1)} %get-tuple-element.94), channel_id=1, source_target_pairs={{0,5},{1,4},{2,7},{3,6},{4,1},{5,0},{6,3},{7,2},{8,13},{9,12},{10,... | collective-permute-start | bytes 786440 | tf_op jit(solution)/shard_map/ppermute | solution.py:306
  294.5 12.7 %collective-permute-start.31 = (bf16[1,64,2048]{2,1,0:T(8,128)(2,1)S(1)}, bf16[1,64,2048]{2,1,0:T(8,128)(2,1)S(1)}, u32[]{:S(2)}, u32[]{:S(2)}) collective-permute-start(bf16[1,64,2048]{2,1,0:T(8,128)(2,1)S(1)} %get-tuple-element.95), channel_id=1, source_target_pairs={{0,4},{1,5},{2,6},{3,7},{4,0},{5,1},{6,2},{7,3},{8,12},{9,13},{10,... | collective-permute-start | bytes 786440 | tf_op jit(solution)/shard_map/ppermute | solution.py:306
  302.1 7.1 %collective-permute-start.30 = (bf16[1,64,2048]{2,1,0:T(8,128)(2,1)S(1)}, bf16[1,64,2048]{2,1,0:T(8,128)(2,1)S(1)}, u32[]{:S(2)}, u32[]{:S(2)}) collective-permute-start(bf16[1,64,2048]{2,1,0:T(8,128)(2,1)S(1)} %get-tuple-element.93), channel_id=1, source_target_pairs={{0,1},{1,0},{2,3},{3,2},{4,5},{5,4},{6,7},{7,6},{8,9},{9,8},{10,11... | collective-permute-start | bytes 786440 | tf_op jit(solution)/shard_map/ppermute | solution.py:306
  303.8 15.7 %collective-permute-start.61 = (bf16[256,1152]{1,0:T(8,128)(2,1)S(1)}, bf16[256,1152]{1,0:T(8,128)(2,1)S(1)}, u32[]{:S(2)}, u32[]{:S(2)}) collective-permute-start(bf16[256,1152]{1,0:T(8,128)(2,1)S(1)} %get-tuple-element.78), channel_id=1, source_target_pairs={{0,6},{2,4},{4,2},{6,0},{1,7},{3,5},{5,3},{7,1},{8,14},{10,12},{12... | collective-permute-start | bytes 1769480 | tf_op jit(solution)/shard_map/ppermute | solution.py:294
  311.6 12.9 %collective-permute-start.35 = (f32[2,64,256]{2,1,0:T(8,128)S(1)}, f32[2,64,256]{2,1,0:T(8,128)S(1)}, u32[]{:S(2)}, u32[]{:S(2)}) collective-permute-start(f32[2,64,256]{2,1,0:T(8,128)S(1)} %get-tuple-element.136), channel_id=1, source_target_pairs={{0,6},{2,4},{4,2},{6,0},{1,7},{3,5},{5,3},{7,1},{8,14},{10,12},{12... | collective-permute-start | bytes 393224 | tf_op jit(solution)/shard_map/ppermute | solution.py:294
  311.7 13.6 %collective-permute-start.34 = (f32[2,64,256]{2,1,0:T(8,128)S(1)}, f32[2,64,256]{2,1,0:T(8,128)S(1)}, u32[]{:S(2)}, u32[]{:S(2)}) collective-permute-start(f32[2,64,256]{2,1,0:T(8,128)S(1)} %get-tuple-element.138), channel_id=1, source_target_pairs={{0,4},{2,6},{4,0},{6,2},{1,5},{3,7},{5,1},{7,3},{8,12},{10,14},{12... | collective-permute-start | bytes 393224 | tf_op jit(solution)/shard_map/ppermute | solution.py:294
  312.9 12.4 %collective-permute-start.33 = (f32[2,64,256]{2,1,0:T(8,128)S(1)}, f32[2,64,256]{2,1,0:T(8,128)S(1)}, u32[]{:S(2)}, u32[]{:S(2)}) collective-permute-start(f32[2,64,256]{2,1,0:T(8,128)S(1)} %get-tuple-element.137), channel_id=1, source_target_pairs={{0,2},{2,0},{4,6},{6,4},{1,3},{3,1},{5,7},{7,5},{8,10},{10,8},{12,... | collective-permute-start | bytes 393224 | tf_op jit(solution)/shard_map/ppermute | solution.py:294
  (80 other events, 572.9 us)
